TPU v7x, 512 devices: a whole 4x4x16 slice. The times are simulated.
512 devices in a mesh: tensor: 8 (over x, core), context: 64 (over y, z).
Axes of the slice: x: 4, y: 4, z: 16, core: 2. Of those that a mesh axis runs over, the one named last changes fastest.
Arguments:
- q_proj: bfloat16 [16384, 8192], P('context', 'tensor'), may hold values from -6 to 6
- k_proj: bfloat16 [16384, 8192], P('context', 'tensor'), may hold values from -6 to 6
- v_proj: bfloat16 [16384, 8192], P('context', 'tensor'), may hold values from -6 to 6
- short_filter: bfloat16 [3, 3, 512], P(None, None, 'tensor'), may hold values from -3.5 to 3.5
- residue: float32 [16, 8192], P(None, 'tensor'), may hold values from -1.5 to 1.5
- decay_rate: float32 [16, 8192], P(None, 'tensor'), may hold values from 0.5 to 512
- out_weight: bfloat16 [4096, 8192], P('context', 'tensor'), may hold values from -0.0625 to 0.0625
Outputs:
- projected: bfloat16 [4096, 16384], P('tensor', 'context')
All inputs are finite; a program needn't handle non-finite values.
Results may differ from a plain program's by a relative error of at most 0.02.
Values may be sent and summed in bfloat16 or wider, within the bound.
A program may use at most 128 MiB of HBM per device.

v0:
```python
import jax
import jax.numpy as jnp
import numpy as np
from jax import lax
from jax.sharding import PartitionSpec as P


def passed_along(block, axis, distance):
    devices = range(lax.axis_size(axis))
    route = [(i - distance, i) for i in devices if i - distance in devices]
    return lax.ppermute(block, axis, route)


def prefix(part, axis, combine, identity):
    place = lax.axis_index(axis)
    gathered = jax.tree.map(lambda a: lax.all_gather(a, axis), part)
    state = jax.tree.map(lambda a, e: jnp.zeros_like(a) + jnp.asarray(e, a.dtype), part, identity)

    def one(lap, state):
        return combine(
            state, jax.tree.map(lambda a: lax.dynamic_index_in_dim(a, lap, 0, False), gathered)
        )

    return lax.fori_loop(0, place, one, state)


def short_pass(extended, filters, group_width):
    tap_count = filters.shape[0]
    length_rows, chan_count = extended.shape
    groups = filters.shape[1]
    widened = jnp.broadcast_to(
        filters.astype(jnp.float32)[:, :, None], (tap_count, groups, group_width)
    ).reshape(tap_count, chan_count)
    out_rows = length_rows - tap_count + 1
    running = jnp.zeros((out_rows, chan_count), jnp.float32)
    for offset in range(tap_count):
        begin = tap_count - 1 - offset
        running = running + widened[offset][None, :] * extended[begin : begin + out_rows].astype(
            jnp.float32
        )
    return running


def compose(earlier, later):
    return (earlier[0] * later[0], earlier[1] * later[0] + later[1])


def per_device(q_proj, k_proj, v_proj, short_filter, residue, decay_rate, out_weight):
    row_count, chan_count = q_proj.shape
    short_taps = short_filter.shape[1]
    group_width = chan_count // short_filter.shape[2]
    lead_rows = short_taps - 1
    q_rim, k_rim, v_rim = passed_along(
        (
            q_proj[row_count - lead_rows :],
            k_proj[row_count - lead_rows :],
            v_proj[row_count - lead_rows :],
        ),
        "context",
        1,
    )
    q_feat = short_pass(
        jnp.concatenate([q_rim, q_proj], axis=0), short_filter[0], group_width
    ).astype(jnp.bfloat16)
    k_feat = short_pass(
        jnp.concatenate([k_rim, k_proj], axis=0), short_filter[1], group_width
    ).astype(jnp.bfloat16)
    v_feat = short_pass(
        jnp.concatenate([v_rim, v_proj], axis=0), short_filter[2], group_width
    ).astype(jnp.bfloat16)
    product = (k_feat.astype(jnp.float32) * v_feat.astype(jnp.float32)).astype(jnp.bfloat16)
    sub_len = 16
    sub_count = row_count // sub_len
    decay_step = decay_rate / (row_count * lax.axis_size("context"))
    mode_scale = residue * jnp.sqrt(2.0 * decay_step)
    offsets = jnp.arange(sub_len).astype(jnp.float32)
    intra_kernel = jnp.sum(
        mode_scale[None] * jnp.exp(-decay_step[None] * offsets[:, None, None]), axis=1
    )
    gap_table = np.arange(sub_len)[None, :] - np.arange(sub_len)[:, None]
    one_hot = (gap_table[:, :, None] == np.arange(sub_len)[None, None, :]).astype(np.float32)
    toeplitz = jnp.einsum(
        "sto,oc->stc", jnp.asarray(one_hot), intra_kernel, precision=lax.Precision.HIGHEST
    )
    local_rows = product.astype(jnp.float32).reshape(sub_count, sub_len, chan_count)
    local_part = jnp.einsum("qsc,stc->qtc", local_rows, toeplitz, precision=lax.Precision.HIGHEST)
    tail_powers = jnp.exp(-decay_step[None] * (sub_len - 1 - offsets)[:, None, None])
    sub_ends = jnp.einsum("qsc,smc->qmc", local_rows, tail_powers, precision=lax.Precision.HIGHEST)
    step_decay = jnp.broadcast_to(jnp.exp(-decay_step * sub_len)[None], sub_ends.shape)
    ignored, carried = lax.associative_scan(compose, (step_decay, sub_ends))
    block_state = carried[-1]
    previous = jnp.concatenate([jnp.zeros_like(carried[:1]), carried[:-1]], axis=0)
    block_decay = jnp.exp(-decay_step * row_count)
    unused, incoming = prefix(
        (block_decay, block_state),
        "context",
        compose,
        (jnp.ones_like(block_decay), jnp.zeros_like(block_state)),
    )
    start_decay = jnp.exp(
        -decay_step[None] * (sub_len * jnp.arange(sub_count)).astype(jnp.float32)[:, None, None]
    )
    prior = previous + start_decay * incoming[None]
    lead_powers = jnp.exp(-decay_step[None] * (offsets + 1.0)[:, None, None])
    carried_part = jnp.einsum(
        "qmc,smc->qsc", prior * mode_scale[None], lead_powers, precision=lax.Precision.HIGHEST
    )
    modal_out = (local_part + carried_part).reshape(row_count, chan_count)
    gated = (q_feat.astype(jnp.float32) * modal_out).astype(jnp.bfloat16)
    partial_terms = lax.dot_general(
        lax.all_gather(out_weight, "context", axis=0, tiled=True),
        gated,
        (((1,), (1,)), ((), ())),
        preferred_element_type=jnp.float32,
    )
    return lax.psum_scatter(
        partial_terms.astype(jnp.bfloat16), "tensor", scatter_dimension=0, tiled=True
    )


def solution(mesh):
    return jax.shard_map(
        per_device,
        mesh=mesh,
        in_specs=(
            P("context", "tensor"),
            P("context", "tensor"),
            P("context", "tensor"),
            P(None, None, "tensor"),
            P(None, "tensor"),
            P(None, "tensor"),
            P("context", "tensor"),
        ),
        out_specs=P("tensor", "context"),
        check_vma=False,
    )
```

profile of v0, /device:TPU:24, one launch (start us, length us, event | category | flops | bytes accessed | tf_op | source)
XLA Modules:
  0.0 510.4 jit_solution(3309768442686726028)
XLA Ops:
  9.0 3.8 collective-permute-start.1
  13.5 3.8 collective-permute-start.2
  19.2 6.2 %copy.86 = f32[16,16,1024]{1,0,2:T(8,128)} copy(f32[16,16,1024]{2,1,0:T(8,128)S(1)} %multiply_exponential_fusion) | data formatting | bytes 2097152 | tf_op jit(solution)/shard_map/exp | solution.py:87
  26.2 4.7 copy.85
  30.9 12.5 %fusion.15 = f32[1024,16,16]{1,2,0:T(8,128)} fusion(f32[16,16,1024]{1,0,2:T(8,128)} %copy.86, bf16[16,16,1024]{1,0,2:T(8,128)(2,1)} %copy.85), kind=kOutput, calls=%fused_computation.72 | convolution fusion | flops 50331648 | bytes 2621440 | tf_op jit(solution)/shard_map/qsc,smc->qmc/dot_general | solution.py:88
  43.3 5.2 %copy.88 = f32[1024,16,16]{0,1,2:T(8,128)S(1)} copy(f32[1024,16,16]{1,2,0:T(8,128)} %fusion.15) | data formatting | bytes 2097152 | tf_op jit(solution)/shard_map/qsc,smc->qmc/dot_general | solution.py:88
  49.2 3.5 pad.122
  55.8 3.8 collective-permute-start
  60.1 3.6 pad.33
  64.0 2.3 slice_add_fusion
  66.3 92.3 %all-gather.9.cloned.1.call-done = f32[1024,1024]{1,0:T(8,128)} async-done(((f32[16,1024]{1,0:T(8,128)}), f32[1024,1024]{1,0:T(8,128)}) %all-gather.9.cloned.1.call-update) | async-done | bytes 4194320 | tf_op jit(solution)/shard_map/all_gather | solution.py:16
  158.5 143.9 %all-gather.5.cloned.1.call-done = f32[64,16,1024]{2,1,0:T(8,128)} async-done(((f32[1,16,1024]{2,1,0:T(8,128)}), f32[64,16,1024]{2,1,0:T(8,128)}) %all-gather.5.cloned.1.call-update) | async-done | bytes 4194320 | tf_op jit(solution)/shard_map/all_gather | solution.py:16
  302.4 44.8 %while.12 = (s32[]{:T(128)}, f32[16,1024]{1,0:T(8,128)S(1)}, s32[]{:T(128)}, f32[64,16,1024]{2,1,0:T(8,128)}, f32[64,16,1024]{2,1,0:T(8,128)}, /*index=5*/s32[]{:T(128)}, s32[]{:T(128)}, s32[]{:T(128)}) while((s32[]{:T(128)}, f32[16,1024]{1,0:T(8,128)S(1)}, s32[]{:T(128)}, f32[64,16,1024]{2,1,0:T(8,128)}, f32[64,16,1024]{2,1,0:T(8,128)}, ...), condition=%wide.region_2.3_spmd, body=%wide.region_1.2_spmd.sunk | while | flops 32773 | bytes 262267 | solution.py:24
  347.2 1.9 add_multiply_fusion
  350.1 6.3 %copy.84 = f32[16,16,1024]{0,1,2:T(8,128)} copy(f32[16,16,1024]{2,1,0:T(8,128)S(1)} %fusion.10) | data formatting | bytes 2097152 | tf_op jit(solution)/shard_map/sto,oc->stc/dot_general | solution.py:82
  356.4 6.1 %copy.89 = f32[16,16,1024]{1,0,2:T(8,128)} copy(f32[16,16,1024]{2,1,0:T(8,128)S(1)} %get-tuple-element.76) | data formatting | bytes 2097152 | tf_op jit(solution)/shard_map/exp | solution.py:104
  362.6 6.2 %copy.90 = f32[16,16,1024]{1,0,2:T(8,128)} copy(f32[16,16,1024]{2,1,0:T(8,128)S(1)} %get-tuple-element.72) | data formatting | bytes 2097152 | tf_op jit(solution)/shard_map/mul | solution.py:106
  368.7 14.6 %fusion.14 = f32[1024,16,16]{2,1,0:T(8,128)} fusion(f32[16,16,1024]{0,1,2:T(8,128)} %copy.84, bf16[16,16,1024]{1,0,2:T(8,128)(2,1)} %copy.85), kind=kOutput, calls=%fused_computation.71 | convolution fusion | flops 50331648 | bytes 2621440 | tf_op jit(solution)/shard_map/qsc,stc->qtc/dot_general | solution.py:86
  383.3 18.0 %add_bitcast_fusion = f32[16,16,1024]{0,1,2:T(8,128)} fusion(f32[1024,16,16]{2,1,0:T(8,128)} %fusion.14, f32[16,16,1024]{1,0,2:T(8,128)S(1)} %copy-done, f32[16,16,1024]{1,0,2:T(8,128)} %copy.90), kind=kOutput, calls=%fused_computation.2 | convolution fusion | flops 50593792 | bytes 4194304 | tf_op jit(solution)/shard_map/qmc,smc->qsc/dot_general | solution.py:105
  401.4 5.5 %copy.91 = f32[16,16,1024]{2,1,0:T(8,128)S(1)} copy(f32[16,16,1024]{0,1,2:T(8,128)} %add_bitcast_fusion) | data formatting | bytes 2097152 | tf_op jit(solution)/shard_map/add | solution.py:108
  407.3 49.2 %all-gather.7.cloned.1.call-done = bf16[4096,1024]{1,0:T(8,128)(2,1)} async-done(((bf16[64,1024]{1,0:T(8,128)(2,1)}), bf16[4096,1024]{1,0:T(8,128)(2,1)}) %all-gather.7.cloned.1.call-update) | async-done | bytes 8388624 | tf_op jit(solution)/shard_map/all_gather | solution.py:111
  456.4 7.1 %fusion = bf16[4096,256]{0,1:T(8,128)(2,1)} fusion(bf16[256,1024]{1,0:T(8,128)(2,1)S(1)} %fusion.1, bf16[4096,1024]{1,0:T(8,128)(2,1)} %all-gather.7.cloned.1.call-done), kind=kOutput, calls=%fused_computation.4 | convolution fusion | flops 2148532224 | bytes 11010048 | tf_op jit(solution)/shard_map/dot_general | solution.py:110
  463.6 38.5 %reduce-scatter.2.cloned.1.call-done = bf16[512,256]{0,1:T(8,128)(2,1)} async-done(((bf16[4096,256]{0,1:T(8,128)(2,1)}), bf16[512,256]{0,1:T(8,128)(2,1)}) %reduce-scatter.2.cloned.1.call-update) | async-done | bytes 262160 | tf_op jit(solution)/shard_map/reduce_scatter | solution.py:116
  502.1 1.8 copy.92
  (125 shorter events, 54.9 us)
Async XLA Ops:
  6.5 18.9 %copy-start.2 = (bf16[256,1024]{1,0:T(8,128)(2,1)S(1)}, bf16[256,1024]{1,0:T(8,128)(2,1)}, u32[]{:S(2)}) copy-start(bf16[256,1024]{1,0:T(8,128)(2,1)} %param.11) | copy-start | bytes 1572868
  6.5 18.9 %copy-start.3 = (bf16[256,1024]{1,0:T(8,128)(2,1)S(1)}, bf16[256,1024]{1,0:T(8,128)(2,1)}, u32[]{:S(2)}) copy-start(bf16[256,1024]{1,0:T(8,128)(2,1)} %param.12) | copy-start | bytes 1572868
  6.5 152.0 %all-gather.9.cloned.1.call-start = ((), (), s32[]{:S(2)}) async-start(), calls=%async_computation.4 | async-start | bytes 4259840 | tf_op jit(solution)/shard_map/all_gather | solution.py:16
  8.2 294.2 %all-gather.5.cloned.1.call-start = ((), (), s32[]{:S(2)}) async-start(), calls=%async_computation.1 | async-start | bytes 4259840 | tf_op jit(solution)/shard_map/all_gather | solution.py:16
  9.0 16.4 %collective-permute-start.1 = (bf16[2,1024]{1,0:T(2,128)(2,1)S(1)}, bf16[2,1024]{1,0:T(2,128)(2,1)S(1)}, u32[]{:S(2)}, u32[]{:S(2)}) collective-permute-start(bf16[2,1024]{1,0:T(2,128)(2,1)S(1)} %slice.217), channel_id=1, source_target_pairs={{0,1},{1,2},{2,3},{3,4},{4,5},{5,6},{6,7},{7,8},{8,9},{9,10},{10,1... | collective-permute-start | bytes 12296 | tf_op jit(solution)/shard_map/ppermute | solution.py:11
  13.5 11.9 %collective-permute-start.2 = (bf16[2,1024]{1,0:T(2,128)(2,1)S(1)}, bf16[2,1024]{1,0:T(2,128)(2,1)S(1)}, u32[]{:S(2)}, u32[]{:S(2)}) collective-permute-start(bf16[2,1024]{1,0:T(2,128)(2,1)S(1)} %slice.227), channel_id=1, source_target_pairs={{0,1},{1,2},{2,3},{3,4},{4,5},{5,6},{6,7},{7,8},{8,9},{9,10},{10,1... | collective-permute-start | bytes 12296 | tf_op jit(solution)/shard_map/ppermute | solution.py:11
  43.3 5.3 %copy-start.1 = (f32[16,1024]{1,0:T(8,128)S(1)}, f32[16,1024]{1,0:T(8,128)}, u32[]{:S(2)}) copy-start(f32[16,1024]{1,0:T(8,128)} %param.15) | copy-start | bytes 196612
  49.2 300.0 %copy-start.5 = (f32[16,16,16]{2,1,0:T(8,128)S(1)}, f32[16,16,16]{2,1,0:T(8,128)}, u32[]{:S(2)}) copy-start(f32[16,16,16]{2,1,0:T(8,128)} %constant.42.clone) | copy-start | bytes 49156
  54.2 402.2 %all-gather.7.cloned.1.call-start = ((), (), s32[]{:S(2)}) async-start(), calls=%async_computation.2 | async-start | bytes 8519680 | tf_op jit(solution)/shard_map/all_gather | solution.py:111
  55.0 447.1 %reduce-scatter.2.cloned.1.call-start = ((), (), s32[]{:S(2)}) async-start(), calls=%async_computation.3 | async-start | bytes 2359296 | tf_op jit(solution)/shard_map/reduce_scatter | solution.py:116
  55.8 351.1 %collective-permute-start = (bf16[2,1024]{1,0:T(2,128)(2,1)S(1)}, bf16[2,1024]{1,0:T(2,128)(2,1)S(1)}, u32[]{:S(2)}, u32[]{:S(2)}) collective-permute-start(bf16[2,1024]{1,0:T(2,128)(2,1)S(1)} %slice.207), channel_id=1, source_target_pairs={{0,1},{1,2},{2,3},{3,4},{4,5},{5,6},{6,7},{7,8},{8,9},{9,10},{10,1... | collective-permute-start | bytes 12296 | tf_op jit(solution)/shard_map/ppermute | solution.py:11
  368.7 14.6 %copy-start = (f32[16,16,1024]{1,0,2:T(8,128)S(1)}, f32[16,16,1024]{1,0,2:T(8,128)}, u32[]{:S(2)}) copy-start(f32[16,16,1024]{1,0,2:T(8,128)} %copy.89) | copy-start | bytes 3145732
  401.4 5.5 %copy-start.4 = (bf16[256,1024]{1,0:T(8,128)(2,1)S(1)}, bf16[256,1024]{1,0:T(8,128)(2,1)}, u32[]{:S(2)}) copy-start(bf16[256,1024]{1,0:T(8,128)(2,1)} %param.10) | copy-start | bytes 1572868
Sparse Core Ops, SparseCore 0:
  10.3 148.2 all-gather.8
  161.5 140.8 all-gather.4
  305.4 151.0 all-gather.6
  463.7 38.3 reduce-scatter.1
where the time goes:
time: 514 us; the launch traced here: 510 us
  waiting for transfers between devices  325 us (63%)
  local copies, waits for them, and re-layouts  54.5 us (11%)
  matrix products  53.2 us (10%)
  other arithmetic  51.9 us (10%)
  between operations  13.4 us (3%)
  starting transfers between devices  11.6 us (2%)
    all_gather x2, waiting for transfers between devices, prefix(): gathered = jax.tree.map(lambda a: lax.all_gather(a, axis), part)  236 us
    all_gather x1, waiting for transfers between devices, per_device(): lax.all_gather(out_weight, 'context', axis=0, tiled=True)  49.2 us
    add x54, other arithmetic, compose(): return (earlier[0] * later[0], earlier[1] * later[0] + later[1])  43.8 us
    reduce_scatter x1, waiting for transfers between devices, per_device(): lax.psum_scatter(partial_terms.astype(jnp.bfloat16), 'tensor', scatter_di...  38.5 us
    dot_general x1, matrix products, per_device(): jnp.einsum('qmc,smc->qsc', prior * mode_scale[None], lead_powers, precisi...  18 us
    dot_general x1, matrix products, per_device(): jnp.einsum('qsc,stc->qtc', local_rows, toeplitz, precision=lax.Precision....  14.6 us
    dot_general x1, matrix products, per_device(): jnp.einsum('qsc,smc->qmc', local_rows, tail_powers, precision=lax.Precisi...  12.5 us
    ppermute x3, starting transfers between devices, passed_along(): return lax.ppermute(block, axis, route)  11.4 us
  transfers between devices with their start and end apart: 7, of which 4 were waited for; matrix products, arithmetic and copies ran while one was open for 29% of the time, Pallas kernels for 0%

commit v1 on v0

v1 whole, which is shorter than its diff:
```python
import functools

import jax
import jax.numpy as jnp
from jax import lax
from jax.experimental import pallas as pl
from jax.experimental.pallas import tpu as pltpu
from jax.sharding import PartitionSpec as P

SPLIT = 4
RING = 16
LANES = 128
SUBL = 8


def front_kernel(q_ref, k_ref, v_ref, rim_ref, filt_ref, decay_ref, q3_ref, p3_ref, end_ref, ext):
    rows = q_ref.shape[0]

    def feature(which, src, lanes):
        ext[0:SUBL, :] = rim_ref[which, :, lanes]
        ext[SUBL : SUBL + rows, :] = src[:, lanes].astype(jnp.float32)
        total = filt_ref[3 * which : 3 * which + 1, lanes] * ext[SUBL : SUBL + rows, :]
        for tap in range(1, 3):
            total = total + filt_ref[3 * which + tap : 3 * which + tap + 1, lanes] * ext[
                SUBL - tap : SUBL - tap + rows, :
            ]
        return total.astype(jnp.bfloat16).astype(jnp.float32)

    for g in range(SUBL):
        lanes = slice(g * LANES, (g + 1) * LANES)
        spread = pl.ds(g, rows, stride=SUBL)
        k_feat = feature(1, k_ref, lanes)
        v_feat = feature(2, v_ref, lanes)
        p3_ref[spread, :] = (k_feat * v_feat).astype(jnp.bfloat16).astype(jnp.float32)
        q3_ref[spread, :] = feature(0, q_ref, lanes)

    modes = decay_ref.shape[0]
    decay = [decay_ref[m] for m in range(modes)]

    def step(lap, state):
        for u in range(8):
            p = p3_ref[pl.ds(pl.multiple_of((lap * 8 + u) * SUBL, SUBL), SUBL), :]
            state = tuple(a * s + p for a, s in zip(decay, state))
        return state

    zero = jnp.zeros((SUBL, LANES), jnp.float32)
    state = lax.fori_loop(0, rows // 8, step, (zero,) * modes)
    for m in range(modes):
        end_ref[m] = state[m]


def back_kernel(q3_ref, p3_ref, start_ref, decay_ref, scale_ref, gated_ref, g3):
    rows = gated_ref.shape[0]
    modes = decay_ref.shape[0]
    decay = [decay_ref[m] for m in range(modes)]
    scale = [scale_ref[m] for m in range(modes)]

    def step(lap, state):
        for u in range(4):
            here = pl.ds(pl.multiple_of((lap * 4 + u) * SUBL, SUBL), SUBL)
            p = p3_ref[here, :]
            state = tuple(a * s + p for a, s in zip(decay, state))
            terms = [c * s for c, s in zip(scale, state)]
            while len(terms) > 1:
                terms = [terms[i] + terms[i + 1] for i in range(0, len(terms), 2)]
            g3[here, :] = q3_ref[here, :] * terms[0]
        return state

    lax.fori_loop(0, rows // 4, step, tuple(start_ref[m] for m in range(modes)))
    for g in range(SUBL):
        gated_ref[:, g * LANES : (g + 1) * LANES] = g3[pl.ds(g, rows, stride=SUBL), :].astype(
            jnp.bfloat16
        )


def vmem_call(kernel, outs, scratch, flops, moved):
    return pl.pallas_call(
        kernel,
        out_shape=outs,
        scratch_shapes=scratch,
        cost_estimate=pl.CostEstimate(flops=flops, bytes_accessed=moved, transcendentals=0),
        compiler_params=pltpu.CompilerParams(vmem_limit_bytes=32 * 1024 * 1024),
    )


def context_shift(block, distance):
    count = lax.axis_size("context")
    return lax.ppermute(
        block, "context", [(i, i + distance) for i in range(count) if i + distance < count]
    )


def y_shift(block, distance):
    count = lax.axis_size("context")
    return lax.ppermute(
        block, "context", [(i, (i + distance * RING) % count) for i in range(count)]
    )


def z_shift(block, distance):
    count = lax.axis_size("context")
    return lax.ppermute(
        block,
        "context",
        [(i, i // RING * RING + (i + distance) % RING) for i in range(count)],
    )


def core_swap(block):
    count = lax.axis_size("tensor")
    return lax.ppermute(block, "tensor", [(i, i ^ 1) for i in range(count)])


def x_shift(block, distance):
    count = lax.axis_size("tensor")
    return lax.ppermute(block, "tensor", [(i, (i + 2 * distance) % count) for i in range(count)])


def pick(block, index, axis=0):
    return lax.dynamic_index_in_dim(block, index, axis, keepdims=False)


def gather_weight(out_weight, y, z):
    rows, chans = out_weight.shape
    sub = rows // SPLIT
    pieces = out_weight.reshape(SPLIT, sub, chans)
    column = jnp.zeros_like(pieces)
    for dy in range(SPLIT):
        piece = pick(pieces, (y + dy) % SPLIT)
        if dy:
            piece = y_shift(piece, dy)
        column = lax.dynamic_update_index_in_dim(column, piece, (y - dy) % SPLIT, 0)
    parts = [(column, 0)]
    ahead = behind = column
    for lap in range(1, RING // 2 + 1):
        ahead = z_shift(ahead, 1)
        parts.append((ahead, -lap))
        if lap < RING // 2:
            behind = z_shift(behind, -1)
            parts.append((behind, lap))
    whole = jnp.zeros((SPLIT, RING, sub, chans), out_weight.dtype)
    for part, offset in parts:
        whole = lax.dynamic_update_index_in_dim(whole, part, (z + offset) % RING, 1)
    return whole.reshape(SPLIT * RING * sub, chans)


def add_over_tensor(partial, x, core):
    blocks = partial.reshape(SPLIT, 2, -1, partial.shape[-1])
    kept = pick(blocks, core, 1).astype(jnp.float32)
    came = core_swap(pick(blocks, 1 - core, 1)).astype(jnp.float32)
    paired = (kept + came).astype(jnp.bfloat16)
    total = pick(paired, x).astype(jnp.float32)
    for dx in range(1, SPLIT):
        total = total + x_shift(pick(paired, (x + dx) % SPLIT), dx).astype(jnp.float32)
    return total.astype(jnp.bfloat16)


def per_device(q_proj, k_proj, v_proj, short_filter, residue, decay_rate, out_weight):
    row_count, chan_count = q_proj.shape
    modes = residue.shape[0]
    taps = short_filter.shape[1]
    group_width = chan_count // short_filter.shape[2]
    place = lax.axis_index("context")
    y, z = place // RING, place % RING
    seat = lax.axis_index("tensor")
    x, core = seat // 2, seat % 2

    rim = jnp.stack([a[row_count - (taps - 1) :] for a in (q_proj, k_proj, v_proj)])
    rim = context_shift(rim, 1).astype(jnp.float32)
    rim = jnp.pad(rim, ((0, 0), (SUBL - (taps - 1), 0), (0, 0)))
    filters = jnp.repeat(
        short_filter.astype(jnp.float32).reshape(3 * taps, -1), group_width, axis=1
    )
    decay_step = (decay_rate / (row_count * lax.axis_size("context"))).reshape(modes, SUBL, LANES)
    mode_scale = residue.reshape(modes, SUBL, LANES) * jnp.sqrt(2.0 * decay_step)
    decay = jnp.exp(-decay_step)

    def block_decay(blocks):
        return jnp.exp(-decay_step * (row_count * blocks))

    wide = jax.ShapeDtypeStruct((row_count * SUBL, LANES), jnp.float32)
    state = jax.ShapeDtypeStruct((modes, SUBL, LANES), jnp.float32)
    elements = row_count * chan_count
    q3, p3, ends = vmem_call(
        front_kernel,
        (wide, wide, state),
        [pltpu.VMEM((row_count + SUBL, LANES), jnp.float32)],
        elements * 60,
        elements * 14,
    )(q_proj, k_proj, v_proj, rim, filters, decay)

    sent = ends.astype(jnp.bfloat16)
    start = context_shift(sent, 1).astype(jnp.float32)
    for d in range(2, 5):
        start = start + block_decay(d - 1) * context_shift(sent, d).astype(jnp.float32)
    for unit in (4, 16):
        sent = start.astype(jnp.bfloat16)
        for d in range(1, 4):
            start = start + block_decay(d * unit) * context_shift(sent, d * unit).astype(
                jnp.float32
            )

    gated = vmem_call(
        back_kernel,
        jax.ShapeDtypeStruct((row_count, chan_count), jnp.bfloat16),
        [pltpu.VMEM((row_count * SUBL, LANES), jnp.float32)],
        elements * 66,
        elements * 10,
    )(q3, p3, start, decay, mode_scale)

    weight = gather_weight(out_weight, y, z)
    share = out_weight.shape[0] // SPLIT
    result = jnp.zeros((share // 2, SPLIT, share, row_count), jnp.bfloat16)
    for dy in (0, 1, 3, 2):
        tokens = y_shift(gated, dy) if dy else gated
        partial = lax.dot_general(
            weight, tokens, (((1,), (1,)), ((), ())), preferred_element_type=jnp.float32
        ).astype(jnp.bfloat16)
        summed = add_over_tensor(partial, x, core)
        if dy:
            summed = y_shift(summed, -dy)
        result = lax.dynamic_update_index_in_dim(
            result, summed.reshape(share // 2, share, row_count), (y + dy) % SPLIT, 1
        )
    return result.reshape(share // 2 * SPLIT * share, row_count)


def solution(mesh):
    return jax.shard_map(
        per_device,
        mesh=mesh,
        in_specs=(
            P("context", "tensor"),
            P("context", "tensor"),
            P("context", "tensor"),
            P(None, None, "tensor"),
            P(None, "tensor"),
            P(None, "tensor"),
            P("context", "tensor"),
        ),
        out_specs=P("tensor", "context"),
        check_vma=False,
    )
```

time: 514 us -> 219 us (0.43)
  waiting for transfers between devices: 325 us -> 39.6 us
  starting transfers between devices: 11.6 us -> 162 us
  other arithmetic: 51.9 us -> 1.56 us
  matrix products: 53.2 us -> 2.99 us
  local copies, waits for them, and re-layouts: 54.5 us -> 4.41 us
  between operations: 13.4 us -> 1.85 us
  Pallas kernels: 0 us -> 5.41 us
    all_gather x3 -> x0, waiting for transfers between devices: 285 us -> none  [the longest x2 236 us: prefix(): gathered = jax.tree.map(lambda a: lax.all_gather(a, axis), part)]
    ppermute x3 -> x51, starting transfers between devices: 11.4 us -> 162 us  [the longest x15 51.2 us: z_shift(): lax.ppermute(block, 'context', [(i, i // RING * RING + (i + distance) % R...]
    dot_general x5 -> x4, matrix products: 53.2 us -> 2.99 us  [per_device(): lax.dot_general(weight, tokens, (((1,), (1,)), ((), ())), preferred_eleme...]
    add x59 -> x1, other arithmetic: 46.2 us -> 0.03 us  [per_device(): start + block_decay(d * unit) * context_shift(sent, d * unit).astype(jnp....]
    ppermute x3 -> x51, waiting for transfers between devices: 0.01 us -> 39.6 us  [the longest x11 21.4 us: context_shift(): lax.ppermute(block, 'context', [(i, i + distance) for i in range(count) i...]
    reduce_scatter x1 -> x0, waiting for transfers between devices: 38.5 us -> none  [per_device(): lax.psum_scatter(partial_terms.astype(jnp.bfloat16), 'tensor', scatter_di...]
    exp x2 -> x0, local copies, waits for them, and re-layouts: 12.3 us -> none  [the longest x1 6.17 us: per_device(): jnp.exp(-decay_step[None] * (sub_len - 1 - offsets)[:, None, None])]
    dot_general x2 -> x0, local copies, waits for them, and re-layouts: 11.5 us -> none  [the longest x1 6.32 us: per_device(): jnp.einsum('sto,oc->stc', jnp.asarray(one_hot), intra_kernel, precision=l...]
  transfers between devices with their start and end apart: 7 -> 51, of which waited for: 4 -> 13; matrix products, arithmetic and copies ran while one was open for 29% -> 3% of each run, Pallas kernels for 0% -> 2%
where the time goes in v1:
time: 219 us; the launch traced here: 217 us
  starting transfers between devices  162 us (74%)
  waiting for transfers between devices  39.6 us (18%)
  Pallas kernels  5.41 us (2%)
  local copies, waits for them, and re-layouts  4.41 us (2%)
  matrix products  2.99 us (1%)
    ppermute x15, starting transfers between devices, z_shift(): lax.ppermute(block, 'context', [(i, i // RING * RING + (i + distance) % R...  51.2 us
    ppermute x12, starting transfers between devices, x_shift(): lax.ppermute(block, 'tensor', [(i, (i + 2 * distance) % count) for i in r...  39.9 us
    ppermute x9, starting transfers between devices, y_shift(): lax.ppermute(block, 'context', [(i, (i + distance * RING) % count) for i...  33 us
    ppermute x11, starting transfers between devices, context_shift(): lax.ppermute(block, 'context', [(i, i + distance) for i in range(count) i...  28.8 us
    ppermute x11, waiting for transfers between devices, context_shift(): lax.ppermute(block, 'context', [(i, i + distance) for i in range(count) i...  21.4 us
    ppermute x15, waiting for transfers between devices, z_shift(): lax.ppermute(block, 'context', [(i, i // RING * RING + (i + distance) % R...  12.5 us
    ppermute x4, starting transfers between devices, core_swap(): return lax.ppermute(block, 'tensor', [(i, i ^ 1) for i in range(count)])  8.66 us
    ppermute x9, waiting for transfers between devices, y_shift(): lax.ppermute(block, 'context', [(i, (i + distance * RING) % count) for i...  5.58 us
  transfers between devices with their start and end apart: 51, of which 13 were waited for; matrix products, arithmetic and copies ran while one was open for 3% of the time, Pallas kernels for 2%

profile of v1, /device:TPU:24, one launch (start us, length us, event | category | flops | bytes accessed | tf_op | source)
XLA Modules:
  0.0 217.3 jit_solution(6653640462296657767)
XLA Ops:
  1.0 7.5 %collective-permute-start = (bf16[16,1024]{1,0:T(8,128)(2,1)S(1)}, bf16[16,1024]{1,0:T(8,128)(2,1)S(1)}, u32[]{:S(2)}, u32[]{:S(2)}) collective-permute-start(bf16[16,1024]{1,0:T(8,128)(2,1)S(1)} %get-tuple-element.29), channel_id=1, source_target_pairs={{0,16},{1,17},{2,18},{3,19},{4,20},{5,21},{6,22},{7,23},{8,24},{9,... | collective-permute-start | bytes 98312 | tf_op jit(solution)/shard_map/ppermute | solution.py:95
  18.8 5.7 %collective-permute-done.18 = bf16[3,2,1024]{2,1,0:T(2,128)(2,1)S(1)} collective-permute-done((bf16[3,2,1024]{2,1,0:T(2,128)(2,1)S(1)}, bf16[3,2,1024]{2,1,0:T(2,128)(2,1)S(1)}, u32[]{:S(2)}, u32[]{:S(2)}) %collective-permute-start.18) | collective-permute-done | bytes 12320 | tf_op jit(solution)/shard_map/ppermute | solution.py:88
  29.8 7.0 %collective-permute-start.21 = (bf16[16,8,128]{2,1,0:T(8,128)(2,1)S(1)}, bf16[16,8,128]{2,1,0:T(8,128)(2,1)S(1)}, u32[]{:S(2)}, u32[]{:S(2)}) collective-permute-start(bf16[16,8,128]{2,1,0:T(8,128)(2,1)S(1)} %convert_element_type.175), channel_id=1, source_target_pairs={{0,3},{1,4},{2,5},{3,6},{4,7},{5,8},{6,9},{7,10},{8,11},{9,12},{10... | collective-permute-start | bytes 98312 | tf_op jit(solution)/shard_map/ppermute | solution.py:88
  36.8 3.9 %collective-permute-start.20 = (bf16[16,8,128]{2,1,0:T(8,128)(2,1)S(1)}, bf16[16,8,128]{2,1,0:T(8,128)(2,1)S(1)}, u32[]{:S(2)}, u32[]{:S(2)}) collective-permute-start(bf16[16,8,128]{2,1,0:T(8,128)(2,1)S(1)} %convert_element_type.175), channel_id=1, source_target_pairs={{0,2},{1,3},{2,4},{3,5},{4,6},{5,7},{6,8},{7,9},{8,10},{9,11},{10,... | collective-permute-start | bytes 98312 | tf_op jit(solution)/shard_map/ppermute | solution.py:88
  57.6 5.1 %collective-permute-start.4 = (bf16[4,16,1024]{2,1,0:T(8,128)(2,1)S(1)}, bf16[4,16,1024]{2,1,0:T(8,128)(2,1)S(1)}, u32[]{:S(2)}, u32[]{:S(2)}) collective-permute-start(bf16[4,16,1024]{2,1,0:T(8,128)(2,1)S(1)} %bitcast_dynamic-update-slice_fusion.16), channel_id=1, source_target_pairs={{0,15},{1,0},{2,1},{3,2},{4,3},{5,4},{6,5},{7,6},{8,7},{9,8},{10,9... | collective-permute-start | bytes 393224 | tf_op jit(solution)/shard_map/ppermute | solution.py:102
  62.7 4.6 %collective-permute-done.24 = bf16[16,8,128]{2,1,0:T(8,128)(2,1)S(1)} collective-permute-done((bf16[16,8,128]{2,1,0:T(8,128)(2,1)S(1)}, bf16[16,8,128]{2,1,0:T(8,128)(2,1)S(1)}, u32[]{:S(2)}, u32[]{:S(2)}) %collective-permute-start.24) | collective-permute-done | bytes 32800 | tf_op jit(solution)/shard_map/ppermute | solution.py:88
  71.6 5.9 %collective-permute-done.28 = bf16[16,8,128]{2,1,0:T(8,128)(2,1)S(1)} collective-permute-done((bf16[16,8,128]{2,1,0:T(8,128)(2,1)S(1)}, bf16[16,8,128]{2,1,0:T(8,128)(2,1)S(1)}, u32[]{:S(2)}, u32[]{:S(2)}) %collective-permute-start.28) | collective-permute-done | bytes 32800 | tf_op jit(solution)/shard_map/ppermute | solution.py:88
  80.2 4.3 %collective-permute-start.33 = (bf16[256,1024]{1,0:T(8,128)(2,1)S(1)}, bf16[256,1024]{1,0:T(8,128)(2,1)S(1)}, u32[]{:S(2)}, u32[]{:S(2)}) collective-permute-start(bf16[256,1024]{1,0:T(8,128)(2,1)S(1)} %shard_map.74), channel_id=1, source_target_pairs={{0,16},{1,17},{2,18},{3,19},{4,20},{5,21},{6,22},{7,23},{8,24},{9,... | collective-permute-start | bytes 1572872 | tf_op jit(solution)/shard_map/ppermute | solution.py:95
  86.4 5.7 %collective-permute-start.45 = (bf16[256,1024]{1,0:T(8,128)(2,1)S(1)}, bf16[256,1024]{1,0:T(8,128)(2,1)S(1)}, u32[]{:S(2)}, u32[]{:S(2)}) collective-permute-start(bf16[256,1024]{1,0:T(8,128)(2,1)S(1)} %shard_map.74), channel_id=1, source_target_pairs={{0,32},{1,33},{2,34},{3,35},{4,36},{5,37},{6,38},{7,39},{8,40},{9,... | collective-permute-start | bytes 1572872 | tf_op jit(solution)/shard_map/ppermute | solution.py:95
  94.1 5.0 %collective-permute-start.6 = (bf16[4,16,1024]{2,1,0:T(8,128)(2,1)S(1)}, bf16[4,16,1024]{2,1,0:T(8,128)(2,1)S(1)}, u32[]{:S(2)}, u32[]{:S(2)}) collective-permute-start(bf16[4,16,1024]{2,1,0:T(8,128)(2,1)S(1)} %collective-permute-done.4), channel_id=1, source_target_pairs={{0,15},{1,0},{2,1},{3,2},{4,3},{5,4},{6,5},{7,6},{8,7},{9,8},{10,9... | collective-permute-start | bytes 393224 | tf_op jit(solution)/shard_map/ppermute | solution.py:102
  102.9 5.1 %collective-permute-start.8 = (bf16[4,16,1024]{2,1,0:T(8,128)(2,1)S(1)}, bf16[4,16,1024]{2,1,0:T(8,128)(2,1)S(1)}, u32[]{:S(2)}, u32[]{:S(2)}) collective-permute-start(bf16[4,16,1024]{2,1,0:T(8,128)(2,1)S(1)} %collective-permute-done.6), channel_id=1, source_target_pairs={{0,15},{1,0},{2,1},{3,2},{4,3},{5,4},{6,5},{7,6},{8,7},{9,8},{10,9... | collective-permute-start | bytes 393224 | tf_op jit(solution)/shard_map/ppermute | solution.py:102
  110.9 5.1 %collective-permute-start.10 = (bf16[4,16,1024]{2,1,0:T(8,128)(2,1)S(1)}, bf16[4,16,1024]{2,1,0:T(8,128)(2,1)S(1)}, u32[]{:S(2)}, u32[]{:S(2)}) collective-permute-start(bf16[4,16,1024]{2,1,0:T(8,128)(2,1)S(1)} %collective-permute-done.8), channel_id=1, source_target_pairs={{0,15},{1,0},{2,1},{3,2},{4,3},{5,4},{6,5},{7,6},{8,7},{9,8},{10,9... | collective-permute-start | bytes 393224 | tf_op jit(solution)/shard_map/ppermute | solution.py:102
  119.0 5.1 %collective-permute-start.12 = (bf16[4,16,1024]{2,1,0:T(8,128)(2,1)S(1)}, bf16[4,16,1024]{2,1,0:T(8,128)(2,1)S(1)}, u32[]{:S(2)}, u32[]{:S(2)}) collective-permute-start(bf16[4,16,1024]{2,1,0:T(8,128)(2,1)S(1)} %collective-permute-done.10), channel_id=1, source_target_pairs={{0,15},{1,0},{2,1},{3,2},{4,3},{5,4},{6,5},{7,6},{8,7},{9,8},{10,9... | collective-permute-start | bytes 393224 | tf_op jit(solution)/shard_map/ppermute | solution.py:102
  127.0 5.1 %collective-permute-start.14 = (bf16[4,16,1024]{2,1,0:T(8,128)(2,1)S(1)}, bf16[4,16,1024]{2,1,0:T(8,128)(2,1)S(1)}, u32[]{:S(2)}, u32[]{:S(2)}) collective-permute-start(bf16[4,16,1024]{2,1,0:T(8,128)(2,1)S(1)} %collective-permute-done.12), channel_id=1, source_target_pairs={{0,15},{1,0},{2,1},{3,2},{4,3},{5,4},{6,5},{7,6},{8,7},{9,8},{10,9... | collective-permute-start | bytes 393224 | tf_op jit(solution)/shard_map/ppermute | solution.py:102
  135.1 5.1 %collective-permute-start.16 = (bf16[4,16,1024]{2,1,0:T(8,128)(2,1)S(1)}, bf16[4,16,1024]{2,1,0:T(8,128)(2,1)S(1)}, u32[]{:S(2)}, u32[]{:S(2)}) collective-permute-start(bf16[4,16,1024]{2,1,0:T(8,128)(2,1)S(1)} %collective-permute-done.14), channel_id=1, source_target_pairs={{0,15},{1,0},{2,1},{3,2},{4,3},{5,4},{6,5},{7,6},{8,7},{9,8},{10,9... | collective-permute-start | bytes 393224 | tf_op jit(solution)/shard_map/ppermute | solution.py:102
  143.2 6.1 %collective-permute-done.17 = bf16[4,16,1024]{2,1,0:T(8,128)(2,1)S(1)} collective-permute-done((bf16[4,16,1024]{2,1,0:T(8,128)(2,1)S(1)}, bf16[4,16,1024]{2,1,0:T(8,128)(2,1)S(1)}, u32[]{:S(2)}, u32[]{:S(2)}) %collective-permute-start.17) | collective-permute-done | bytes 131104 | tf_op jit(solution)/shard_map/ppermute | solution.py:102
  161.3 4.7 %collective-permute-start.32 = (bf16[128,256]{1,0:T(8,128)(2,1)S(1)}, bf16[128,256]{1,0:T(8,128)(2,1)S(1)}, u32[]{:S(2)}, u32[]{:S(2)}) collective-permute-start(bf16[128,256]{1,0:T(8,128)(2,1)S(1)} %get-tuple-element.25), channel_id=1, source_target_pairs={{0,384},{64,448},{128,0},{192,64},{256,128},{320,192},{384,256},{4... | collective-permute-start | bytes 196616 | tf_op jit(solution)/shard_map/ppermute | solution.py:116
  171.9 3.7 %collective-permute-start.36 = (bf16[128,256]{1,0:T(8,128)(2,1)S(1)}, bf16[128,256]{1,0:T(8,128)(2,1)S(1)}, u32[]{:S(2)}, u32[]{:S(2)}) collective-permute-start(bf16[128,256]{1,0:T(8,128)(2,1)S(1)} %get-tuple-element.23), channel_id=1, source_target_pairs={{0,256},{64,320},{128,384},{192,448},{256,0},{320,64},{384,128},{4... | collective-permute-start | bytes 196616 | tf_op jit(solution)/shard_map/ppermute | solution.py:116
  179.0 3.9 %collective-permute-start.43 = (bf16[128,256]{1,0:T(8,128)(2,1)S(1)}, bf16[128,256]{1,0:T(8,128)(2,1)S(1)}, u32[]{:S(2)}, u32[]{:S(2)}) collective-permute-start(bf16[128,256]{1,0:T(8,128)(2,1)S(1)} %get-tuple-element.19), channel_id=1, source_target_pairs={{0,384},{64,448},{128,0},{192,64},{256,128},{320,192},{384,256},{4... | collective-permute-start | bytes 196616 | tf_op jit(solution)/shard_map/ppermute | solution.py:116
  188.2 4.3 %collective-permute-start.49 = (bf16[128,256]{1,0:T(8,128)(2,1)S(1)}, bf16[128,256]{1,0:T(8,128)(2,1)S(1)}, u32[]{:S(2)}, u32[]{:S(2)}) collective-permute-start(bf16[128,256]{1,0:T(8,128)(2,1)S(1)} %get-tuple-element.16), channel_id=1, source_target_pairs={{0,384},{64,448},{128,0},{192,64},{256,128},{320,192},{384,256},{4... | collective-permute-start | bytes 196616 | tf_op jit(solution)/shard_map/ppermute | solution.py:116
  192.5 3.7 %collective-permute-start.48 = (bf16[128,256]{1,0:T(8,128)(2,1)S(1)}, bf16[128,256]{1,0:T(8,128)(2,1)S(1)}, u32[]{:S(2)}, u32[]{:S(2)}) collective-permute-start(bf16[128,256]{1,0:T(8,128)(2,1)S(1)} %get-tuple-element.17), channel_id=1, source_target_pairs={{0,256},{64,320},{128,384},{192,448},{256,0},{320,64},{384,128},{4... | collective-permute-start | bytes 196616 | tf_op jit(solution)/shard_map/ppermute | solution.py:116
  198.2 3.6 %collective-permute-start.30 = (bf16[128,256]{1,0:T(8,128)(2,1)S(1)}, bf16[128,256]{1,0:T(8,128)(2,1)S(1)}, u32[]{:S(2)}, u32[]{:S(2)}) collective-permute-start(bf16[128,256]{1,0:T(8,128)(2,1)S(1)} %get-tuple-element.24), channel_id=1, source_target_pairs={{0,128},{64,192},{128,256},{192,320},{256,384},{320,448},{384,0},{... | collective-permute-start | bytes 196616 | tf_op jit(solution)/shard_map/ppermute | solution.py:116
  204.1 4.8 %collective-permute-start.44 = (bf16[128,256]{1,0:T(8,128)(2,1)S(1)}, bf16[128,256]{1,0:T(8,128)(2,1)S(1)}, u32[]{:S(2)}, u32[]{:S(2)}) collective-permute-start(bf16[128,256]{1,0:T(8,128)(2,1)S(1)} %fusion.9), channel_id=1, source_target_pairs={{0,16},{1,17},{2,18},{3,19},{4,20},{5,21},{6,22},{7,23},{8,24},{9,... | collective-permute-start | bytes 196616 | tf_op jit(solution)/shard_map/ppermute | solution.py:95
  211.1 5.6 %collective-permute-done.50 = bf16[128,256]{1,0:T(8,128)(2,1)S(1)} collective-permute-done((bf16[128,256]{1,0:T(8,128)(2,1)S(1)}, bf16[128,256]{1,0:T(8,128)(2,1)S(1)}, u32[]{:S(2)}, u32[]{:S(2)}) %collective-permute-start.50) | collective-permute-done | bytes 65568 | tf_op jit(solution)/shard_map/ppermute | solution.py:95
  (160 shorter events, 94.9 us)
Async XLA Ops:
  1.0 35.8 %collective-permute-start = (bf16[16,1024]{1,0:T(8,128)(2,1)S(1)}, bf16[16,1024]{1,0:T(8,128)(2,1)S(1)}, u32[]{:S(2)}, u32[]{:S(2)}) collective-permute-start(bf16[16,1024]{1,0:T(8,128)(2,1)S(1)} %get-tuple-element.29), channel_id=1, source_target_pairs={{0,16},{1,17},{2,18},{3,19},{4,20},{5,21},{6,22},{7,23},{8,24},{9,... | collective-permute-start | bytes 98312 | tf_op jit(solution)/shard_map/ppermute | solution.py:95
  8.5 32.2 %collective-permute-start.1 = (bf16[16,1024]{1,0:T(8,128)(2,1)S(1)}, bf16[16,1024]{1,0:T(8,128)(2,1)S(1)}, u32[]{:S(2)}, u32[]{:S(2)}) collective-permute-start(bf16[16,1024]{1,0:T(8,128)(2,1)S(1)} %get-tuple-element.28), channel_id=1, source_target_pairs={{0,32},{1,33},{2,34},{3,35},{4,36},{5,37},{6,38},{7,39},{8,40},{9,... | collective-permute-start | bytes 98312 | tf_op jit(solution)/shard_map/ppermute | solution.py:95
  10.4 45.2 %collective-permute-start.2 = (bf16[16,1024]{1,0:T(8,128)(2,1)S(1)}, bf16[16,1024]{1,0:T(8,128)(2,1)S(1)}, u32[]{:S(2)}, u32[]{:S(2)}) collective-permute-start(bf16[16,1024]{1,0:T(8,128)(2,1)S(1)} %get-tuple-element.27), channel_id=1, source_target_pairs={{0,48},{1,49},{2,50},{3,51},{4,52},{5,53},{6,54},{7,55},{8,56},{9,... | collective-permute-start | bytes 98312 | tf_op jit(solution)/shard_map/ppermute | solution.py:95
  27.3 16.3 %collective-permute-start.22 = (bf16[16,8,128]{2,1,0:T(8,128)(2,1)S(1)}, bf16[16,8,128]{2,1,0:T(8,128)(2,1)S(1)}, u32[]{:S(2)}, u32[]{:S(2)}) collective-permute-start(bf16[16,8,128]{2,1,0:T(8,128)(2,1)S(1)} %convert_element_type.175), channel_id=1, source_target_pairs={{0,4},{1,5},{2,6},{3,7},{4,8},{5,9},{6,10},{7,11},{8,12},{9,13},{1... | collective-permute-start | bytes 98312 | tf_op jit(solution)/shard_map/ppermute | solution.py:88
  29.8 13.8 %collective-permute-start.21 = (bf16[16,8,128]{2,1,0:T(8,128)(2,1)S(1)}, bf16[16,8,128]{2,1,0:T(8,128)(2,1)S(1)}, u32[]{:S(2)}, u32[]{:S(2)}) collective-permute-start(bf16[16,8,128]{2,1,0:T(8,128)(2,1)S(1)} %convert_element_type.175), channel_id=1, source_target_pairs={{0,3},{1,4},{2,5},{3,6},{4,7},{5,8},{6,9},{7,10},{8,11},{9,12},{10... | collective-permute-start | bytes 98312 | tf_op jit(solution)/shard_map/ppermute | solution.py:88
  48.8 13.9 %collective-permute-start.25 = (bf16[16,8,128]{2,1,0:T(8,128)(2,1)S(1)}, bf16[16,8,128]{2,1,0:T(8,128)(2,1)S(1)}, u32[]{:S(2)}, u32[]{:S(2)}) collective-permute-start(bf16[16,8,128]{2,1,0:T(8,128)(2,1)S(1)} %get-tuple-element.13), channel_id=1, source_target_pairs={{0,12},{1,13},{2,14},{3,15},{4,16},{5,17},{6,18},{7,19},{8,20},{9,... | collective-permute-start | bytes 98312 | tf_op jit(solution)/shard_map/ppermute | solution.py:88
  50.8 16.6 %collective-permute-start.24 = (bf16[16,8,128]{2,1,0:T(8,128)(2,1)S(1)}, bf16[16,8,128]{2,1,0:T(8,128)(2,1)S(1)}, u32[]{:S(2)}, u32[]{:S(2)}) collective-permute-start(bf16[16,8,128]{2,1,0:T(8,128)(2,1)S(1)} %get-tuple-element.13), channel_id=1, source_target_pairs={{0,8},{1,9},{2,10},{3,11},{4,12},{5,13},{6,14},{7,15},{8,16},{9,17... | collective-permute-start | bytes 98312 | tf_op jit(solution)/shard_map/ppermute | solution.py:88
  53.7 13.7 %collective-permute-start.23 = (bf16[16,8,128]{2,1,0:T(8,128)(2,1)S(1)}, bf16[16,8,128]{2,1,0:T(8,128)(2,1)S(1)}, u32[]{:S(2)}, u32[]{:S(2)}) collective-permute-start(bf16[16,8,128]{2,1,0:T(8,128)(2,1)S(1)} %get-tuple-element.13), channel_id=1, source_target_pairs={{0,4},{1,5},{2,6},{3,7},{4,8},{5,9},{6,10},{7,11},{8,12},{9,13},{1... | collective-permute-start | bytes 98312 | tf_op jit(solution)/shard_map/ppermute | solution.py:88
  55.6 36.5 %collective-permute-start.3 = (bf16[4,16,1024]{2,1,0:T(8,128)(2,1)S(1)}, bf16[4,16,1024]{2,1,0:T(8,128)(2,1)S(1)}, u32[]{:S(2)}, u32[]{:S(2)}) collective-permute-start(bf16[4,16,1024]{2,1,0:T(8,128)(2,1)S(1)} %bitcast_dynamic-update-slice_fusion.16), channel_id=1, source_target_pairs={{0,1},{1,2},{2,3},{3,4},{4,5},{5,6},{6,7},{7,8},{8,9},{9,10},{10,1... | collective-permute-start | bytes 393224 | tf_op jit(solution)/shard_map/ppermute | solution.py:102
  57.6 36.6 %collective-permute-start.4 = (bf16[4,16,1024]{2,1,0:T(8,128)(2,1)S(1)}, bf16[4,16,1024]{2,1,0:T(8,128)(2,1)S(1)}, u32[]{:S(2)}, u32[]{:S(2)}) collective-permute-start(bf16[4,16,1024]{2,1,0:T(8,128)(2,1)S(1)} %bitcast_dynamic-update-slice_fusion.16), channel_id=1, source_target_pairs={{0,15},{1,0},{2,1},{3,2},{4,3},{5,4},{6,5},{7,6},{8,7},{9,8},{10,9... | collective-permute-start | bytes 393224 | tf_op jit(solution)/shard_map/ppermute | solution.py:102
  67.4 10.1 %collective-permute-start.28 = (bf16[16,8,128]{2,1,0:T(8,128)(2,1)S(1)}, bf16[16,8,128]{2,1,0:T(8,128)(2,1)S(1)}, u32[]{:S(2)}, u32[]{:S(2)}) collective-permute-start(bf16[16,8,128]{2,1,0:T(8,128)(2,1)S(1)} %get-tuple-element.11), channel_id=1, source_target_pairs={{0,48},{1,49},{2,50},{3,51},{4,52},{5,53},{6,54},{7,55},{8,56},{9,... | collective-permute-start | bytes 98312 | tf_op jit(solution)/shard_map/ppermute | solution.py:88
  80.2 71.8 %collective-permute-start.33 = (bf16[256,1024]{1,0:T(8,128)(2,1)S(1)}, bf16[256,1024]{1,0:T(8,128)(2,1)S(1)}, u32[]{:S(2)}, u32[]{:S(2)}) collective-permute-start(bf16[256,1024]{1,0:T(8,128)(2,1)S(1)} %shard_map.74), channel_id=1, source_target_pairs={{0,16},{1,17},{2,18},{3,19},{4,20},{5,21},{6,22},{7,23},{8,24},{9,... | collective-permute-start | bytes 1572872 | tf_op jit(solution)/shard_map/ppermute | solution.py:95
  84.5 70.8 %collective-permute-start.39 = (bf16[256,1024]{1,0:T(8,128)(2,1)S(1)}, bf16[256,1024]{1,0:T(8,128)(2,1)S(1)}, u32[]{:S(2)}, u32[]{:S(2)}) collective-permute-start(bf16[256,1024]{1,0:T(8,128)(2,1)S(1)} %shard_map.74), channel_id=1, source_target_pairs={{0,48},{1,49},{2,50},{3,51},{4,52},{5,53},{6,54},{7,55},{8,56},{9,... | collective-permute-start | bytes 1572872 | tf_op jit(solution)/shard_map/ppermute | solution.py:95
  86.4 71.6 %collective-permute-start.45 = (bf16[256,1024]{1,0:T(8,128)(2,1)S(1)}, bf16[256,1024]{1,0:T(8,128)(2,1)S(1)}, u32[]{:S(2)}, u32[]{:S(2)}) collective-permute-start(bf16[256,1024]{1,0:T(8,128)(2,1)S(1)} %shard_map.74), channel_id=1, source_target_pairs={{0,32},{1,33},{2,34},{3,35},{4,36},{5,37},{6,38},{7,39},{8,40},{9,... | collective-permute-start | bytes 1572872 | tf_op jit(solution)/shard_map/ppermute | solution.py:95
  150.1 11.1 %collective-permute-start.29 = (bf16[4,128,256]{2,1,0:T(8,128)(2,1)S(1)}, bf16[4,128,256]{2,1,0:T(8,128)(2,1)S(1)}, u32[]{:S(2)}, u32[]{:S(2)}) collective-permute-start(bf16[4,128,256]{2,1,0:T(8,128)(2,1)S(1)} %dynamic-slice_bitcast_fusion.3), channel_id=1, source_target_pairs={{0,64},{64,0},{128,192},{192,128},{256,320},{320,256},{384,448},{4... | collective-permute-start | bytes 786440 | tf_op jit(solution)/shard_map/ppermute | solution.py:111
  152.8 15.9 %collective-permute-start.34 = (bf16[4,128,256]{2,1,0:T(8,128)(2,1)S(1)}, bf16[4,128,256]{2,1,0:T(8,128)(2,1)S(1)}, u32[]{:S(2)}, u32[]{:S(2)}) collective-permute-start(bf16[4,128,256]{2,1,0:T(8,128)(2,1)S(1)} %dynamic-slice_bitcast_fusion.2), channel_id=1, source_target_pairs={{0,64},{64,0},{128,192},{192,128},{256,320},{320,256},{384,448},{4... | collective-permute-start | bytes 786440 | tf_op jit(solution)/shard_map/ppermute | solution.py:111
  156.0 15.8 %collective-permute-start.40 = (bf16[4,128,256]{2,1,0:T(8,128)(2,1)S(1)}, bf16[4,128,256]{2,1,0:T(8,128)(2,1)S(1)}, u32[]{:S(2)}, u32[]{:S(2)}) collective-permute-start(bf16[4,128,256]{2,1,0:T(8,128)(2,1)S(1)} %dynamic-slice_bitcast_fusion.1), channel_id=1, source_target_pairs={{0,64},{64,0},{128,192},{192,128},{256,320},{320,256},{384,448},{4... | collective-permute-start | bytes 786440 | tf_op jit(solution)/shard_map/ppermute | solution.py:111
  158.8 16.9 %collective-permute-start.46 = (bf16[4,128,256]{2,1,0:T(8,128)(2,1)S(1)}, bf16[4,128,256]{2,1,0:T(8,128)(2,1)S(1)}, u32[]{:S(2)}, u32[]{:S(2)}) collective-permute-start(bf16[4,128,256]{2,1,0:T(8,128)(2,1)S(1)} %dynamic-slice_bitcast_fusion), channel_id=1, source_target_pairs={{0,64},{64,0},{128,192},{192,128},{256,320},{320,256},{384,448},{4... | collective-permute-start | bytes 786440 | tf_op jit(solution)/shard_map/ppermute | solution.py:111
  161.3 47.7 %collective-permute-start.32 = (bf16[128,256]{1,0:T(8,128)(2,1)S(1)}, bf16[128,256]{1,0:T(8,128)(2,1)S(1)}, u32[]{:S(2)}, u32[]{:S(2)}) collective-permute-start(bf16[128,256]{1,0:T(8,128)(2,1)S(1)} %get-tuple-element.25), channel_id=1, source_target_pairs={{0,384},{64,448},{128,0},{192,64},{256,128},{320,192},{384,256},{4... | collective-permute-start | bytes 196616 | tf_op jit(solution)/shard_map/ppermute | solution.py:116
  166.0 44.9 %collective-permute-start.31 = (bf16[128,256]{1,0:T(8,128)(2,1)S(1)}, bf16[128,256]{1,0:T(8,128)(2,1)S(1)}, u32[]{:S(2)}, u32[]{:S(2)}) collective-permute-start(bf16[128,256]{1,0:T(8,128)(2,1)S(1)} %get-tuple-element.26), channel_id=1, source_target_pairs={{0,256},{64,320},{128,384},{192,448},{256,0},{320,64},{384,128},{4... | collective-permute-start | bytes 196616 | tf_op jit(solution)/shard_map/ppermute | solution.py:116
  168.8 10.1 %collective-permute-start.37 = (bf16[128,256]{1,0:T(8,128)(2,1)S(1)}, bf16[128,256]{1,0:T(8,128)(2,1)S(1)}, u32[]{:S(2)}, u32[]{:S(2)}) collective-permute-start(bf16[128,256]{1,0:T(8,128)(2,1)S(1)} %get-tuple-element.22), channel_id=1, source_target_pairs={{0,384},{64,448},{128,0},{192,64},{256,128},{320,192},{384,256},{4... | collective-permute-start | bytes 196616 | tf_op jit(solution)/shard_map/ppermute | solution.py:116
  171.9 11.0 %collective-permute-start.36 = (bf16[128,256]{1,0:T(8,128)(2,1)S(1)}, bf16[128,256]{1,0:T(8,128)(2,1)S(1)}, u32[]{:S(2)}, u32[]{:S(2)}) collective-permute-start(bf16[128,256]{1,0:T(8,128)(2,1)S(1)} %get-tuple-element.23), channel_id=1, source_target_pairs={{0,256},{64,320},{128,384},{192,448},{256,0},{320,64},{384,128},{4... | collective-permute-start | bytes 196616 | tf_op jit(solution)/shard_map/ppermute | solution.py:116
  185.4 10.9 %collective-permute-start.41 = (bf16[128,256]{1,0:T(8,128)(2,1)S(1)}, bf16[128,256]{1,0:T(8,128)(2,1)S(1)}, u32[]{:S(2)}, u32[]{:S(2)}) collective-permute-start(bf16[128,256]{1,0:T(8,128)(2,1)S(1)} %get-tuple-element.18), channel_id=1, source_target_pairs={{0,128},{64,192},{128,256},{192,320},{256,384},{320,448},{384,0},{... | collective-permute-start | bytes 196616 | tf_op jit(solution)/shard_map/ppermute | solution.py:116
  198.2 12.7 %collective-permute-start.30 = (bf16[128,256]{1,0:T(8,128)(2,1)S(1)}, bf16[128,256]{1,0:T(8,128)(2,1)S(1)}, u32[]{:S(2)}, u32[]{:S(2)}) collective-permute-start(bf16[128,256]{1,0:T(8,128)(2,1)S(1)} %get-tuple-element.24), channel_id=1, source_target_pairs={{0,128},{64,192},{128,256},{192,320},{256,384},{320,448},{384,0},{... | collective-permute-start | bytes 196616 | tf_op jit(solution)/shard_map/ppermute | solution.py:116
  (32 other events, 321.0 us)

commit v2 on v0

v2 whole, which is shorter than its diff:
```python
import functools

import jax
import jax.numpy as jnp
from jax import lax
from jax.experimental import pallas as pl
from jax.experimental.pallas import tpu as pltpu
from jax.sharding import PartitionSpec as P

SPLIT = 4
RING = 16
LANES = 128
SUBL = 8
UP, DOWN = 6, 9
FAR = (1, 2, 3, 4, 8, 12)
COPIES = 128


def mixer_kernel(
    total_rows, q_ref, k_ref, v_ref, filt_ref, residue_ref, rate_ref, w_ref, out_ref,
    ext, head, p3, q3, g3, wide, rim_out, rim_in, st_out, st_in, whole, tokens,
    part, swapped, paired, crossed, summed, homed, send_sem, recv_sem,
):
    rows = q_ref.shape[0]
    modes = rate_ref.shape[0]
    sub = w_ref.shape[1]
    place = lax.axis_index("context")
    blocks = lax.axis_size("context")
    y, z = place // RING, place % RING
    seat = lax.axis_index("tensor")
    x, core = seat // 2, seat % 2

    def on_context(distance):
        return {"context": lax.rem(place + (distance + blocks), blocks)}

    def on_ring(distance):
        return {"context": y * RING + lax.rem(z + (distance + RING), RING)}

    def on_x(distance):
        return {"tensor": lax.rem(seat + 2 * distance, 2 * SPLIT)}

    other_core = {"tensor": x * 2 + (1 - core)}
    peers = [on_context(d) for d in FAR] + [on_context(-d) for d in FAR]
    peers += [on_context(d * RING) for d in range(1, SPLIT)]
    peers += [on_ring(1), on_ring(-1), other_core]
    peers += [on_x(d) for d in range(1, SPLIT)]
    barrier = pltpu.get_barrier_semaphore()
    for peer in peers:
        pl.semaphore_signal(barrier, inc=1, device_id=peer, device_id_type=pl.DeviceIdType.MESH)

    started = []

    def send(src, dst, peer):
        index = len(started)
        copy = pltpu.make_async_remote_copy(
            src_ref=src,
            dst_ref=dst,
            send_sem=send_sem.at[index],
            recv_sem=recv_sem.at[index],
            device_id=peer,
            device_id_type=pl.DeviceIdType.MESH,
        )
        copy.start()
        started.append(copy)
        return copy

    rim_out[...] = jnp.zeros_like(rim_out)
    for n, src in enumerate((q_ref, k_ref, v_ref)):
        rim_out[2 * n : 2 * n + 2, :] = src[rows - 16 : rows, :].astype(jnp.float32)[14:16]

    def feature(which, src, lanes):
        ext[0:SUBL, :] = jnp.zeros((SUBL, LANES), jnp.float32)
        ext[SUBL : SUBL + rows, :] = src[:, lanes].astype(jnp.float32)
        total = filt_ref[3 * which : 3 * which + 1, lanes] * ext[SUBL : SUBL + rows, :]
        for tap in range(1, 3):
            total = total + filt_ref[3 * which + tap : 3 * which + tap + 1, lanes] * ext[
                SUBL - tap : SUBL - tap + rows, :
            ]
        return total.astype(jnp.bfloat16).astype(jnp.float32)

    for g in range(SUBL):
        lanes = slice(g * LANES, (g + 1) * LANES)
        spread = pl.ds(g, rows, stride=SUBL)
        k_feat = feature(1, k_ref, lanes)
        v_feat = feature(2, v_ref, lanes)
        p3[spread, :] = (k_feat * v_feat).astype(jnp.bfloat16).astype(jnp.float32)
        q3[spread, :] = feature(0, q_ref, lanes)
        wide[0, pl.ds(g, modes, stride=SUBL), :] = rate_ref[:, lanes] / total_rows
        wide[1, pl.ds(g, modes, stride=SUBL), :] = residue_ref[:, lanes]
    decay_step = wide[0]
    wide[2] = jnp.exp(-decay_step)
    wide[1] = wide[1] * jnp.sqrt(2.0 * decay_step)

    def mode_rows(slot):
        return [wide[slot, m * SUBL : (m + 1) * SUBL, :] for m in range(modes)]

    def run(first, last, state, gate):
        decay = mode_rows(2)
        scale = mode_rows(1) if gate else None
        unroll = 4

        def step(lap, state):
            for u in range(unroll):
                at = pl.ds(pl.multiple_of((lap * unroll + u) * SUBL, SUBL), SUBL)
                p = p3[at, :]
                state = tuple(a * s + p for a, s in zip(decay, state))
                if gate:
                    terms = [c * s for c, s in zip(scale, state)]
                    while len(terms) > 1:
                        terms = [terms[i] + terms[i + 1] for i in range(0, len(terms), 2)]
                    g3[at, :] = q3[at, :] * terms[0]
            return state

        return lax.fori_loop(first // unroll, last // unroll, step, state)

    zero = jnp.zeros((SUBL, LANES), jnp.float32)
    body_end = run(SUBL, rows, (zero,) * modes, False)
    whole[z, y] = w_ref[y]

    pl.semaphore_wait(barrier, len(peers))
    rim_copy = send(rim_out, rim_in, on_context(1))
    column = [None] + [
        send(w_ref.at[lax.rem(y + dy, SPLIT)], whole.at[z, y], on_context(dy * RING))
        for dy in range(1, SPLIT)
    ]

    def from_y(dy):
        return lax.rem(y + (SPLIT - dy), SPLIT)

    up = [[None] * SPLIT for _ in range(UP + 1)]
    down = [[None] * SPLIT for _ in range(DOWN + 1)]

    def ring(lap):
        for dy in range(SPLIT):
            source = from_y(dy)
            if lap == 0:
                if dy:
                    column[dy].wait_recv()
            for laps, count, sign in ((up, UP, 1), (down, DOWN, -1)):
                if lap > count:
                    continue
                if lap:
                    laps[lap][dy].wait_recv()
                if lap < count:
                    slot = whole.at[lax.rem(z + (RING - sign * lap), RING), source]
                    block = w_ref.at[y] if lap == 0 and dy == 0 else slot
                    laps[lap + 1][dy] = send(block, slot, on_ring(sign))

    rim_copy.wait_recv()
    rim = jnp.where(place > 0, rim_in[...], 0.0)
    feats = []
    for n, src in enumerate((q_ref, k_ref, v_ref)):
        head[0:SUBL, :] = jnp.zeros((SUBL, head.shape[1]), jnp.float32)
        head[SUBL - 2 : SUBL, :] = rim[2 * n : 2 * n + 2]
        head[SUBL : 2 * SUBL, :] = src[0:16, :].astype(jnp.float32)[0:SUBL]
        total = filt_ref[3 * n : 3 * n + 1, :] * head[SUBL : 2 * SUBL, :]
        for tap in range(1, 3):
            total = total + filt_ref[3 * n + tap : 3 * n + tap + 1, :] * head[
                SUBL - tap : 2 * SUBL - tap, :
            ]
        feats.append(total.astype(jnp.bfloat16).astype(jnp.float32))
    first_product = (feats[1] * feats[2]).astype(jnp.bfloat16).astype(jnp.float32)
    for g in range(SUBL):
        lanes = slice(g * LANES, (g + 1) * LANES)
        p3[pl.ds(g, SUBL, stride=SUBL), :] = first_product[:, lanes]
        q3[pl.ds(g, SUBL, stride=SUBL), :] = feats[0][:, lanes]
    head_end = jnp.concatenate(run(0, SUBL, (zero,) * modes, False), axis=0)
    state = jnp.concatenate(body_end, axis=0) + jnp.exp(-decay_step * (rows - SUBL)) * head_end

    def start_round(slot, first_copy, distances):
        return [
            send(st_out.at[slot], st_in.at[first_copy + i], on_context(d))
            for i, d in enumerate(distances)
        ]

    def end_round(copies, first_copy, distances, lead, total):
        for i, d in enumerate(distances):
            copies[i].wait_recv()
            came = jnp.where(place >= d, st_in[first_copy + i].astype(jnp.float32), 0.0)
            if d != lead:
                came = came * jnp.exp(-decay_step * (rows * (d - lead)))
            total = came if total is None else total + came
        return total

    st_out[0] = state.astype(jnp.bfloat16)
    near = (1, 2, 3, 4)
    copies = start_round(0, 0, near)
    ring(0)
    ring(1)
    state = end_round(copies, 0, near, 1, None)
    st_out[1] = state.astype(jnp.bfloat16)
    middle = (4, 8, 12)
    copies = start_round(1, 4, middle)
    ring(2)
    ring(3)
    ring(4)
    state = end_round(copies, 4, middle, 0, state)
    st_out[2] = state.astype(jnp.bfloat16)
    distant = (16, 32, 48)
    copies = start_round(2, 7, distant)
    ring(5)
    state = end_round(copies, 7, distant, 0, state)

    run(0, rows, tuple(state[m * SUBL : (m + 1) * SUBL] for m in range(modes)), True)
    for g in range(SUBL):
        gated = g3[pl.ds(g, rows, stride=SUBL), :].astype(jnp.bfloat16)
        tokens[0, 0, :, g * LANES : (g + 1) * LANES] = gated[: rows // 2]
        tokens[0, 1, :, g * LANES : (g + 1) * LANES] = gated[rows // 2 :]

    from_below, from_above = on_context(RING), on_context(-RING)
    low = [send(tokens.at[0, h], tokens.at[1, h], from_below) for h in (0, 1)]
    high = [send(tokens.at[0, h], tokens.at[3, h], from_above) for h in (1, 0)]
    ring(6)
    ring(7)
    low[0].wait_recv()
    across = [send(tokens.at[1, 0], tokens.at[2, 0], from_below)]
    high[0].wait_recv()
    across.append(send(tokens.at[3, 1], tokens.at[2, 1], from_above))
    ring(8)
    ring(9)

    share = SUBL * sub

    def multiply(dy):
        rhs = tokens[dy].reshape(rows, -1)
        for half in range(2):
            lhs = whole[half * SUBL : (half + 1) * SUBL].reshape(SPLIT * share, -1)
            terms = lax.dot_general(
                lhs, rhs, (((1,), (1,)), ((), ())), preferred_element_type=jnp.float32
            ).astype(jnp.bfloat16)
            terms = terms.reshape(SUBL, SPLIT, sub, rows)
            for col in range(SPLIT):
                part[dy, half, col] = terms[:, col].reshape(share, rows)
        return send(part.at[dy, 1 - core], swapped.at[dy], other_core)

    def pair(dy, copy):
        copy.wait_recv()
        both = part[dy, core].astype(jnp.float32) + swapped[dy].astype(jnp.float32)
        paired[dy] = both.astype(jnp.bfloat16)
        return [
            send(paired.at[dy, lax.rem(x + dx, SPLIT)], crossed.at[dy, dx - 1], on_x(dx))
            for dx in range(1, SPLIT)
        ]

    def finish(dy, copies):
        total = paired[dy, x].astype(jnp.float32)
        for dx in range(1, SPLIT):
            copies[dx - 1].wait_recv()
            total = total + crossed[dy, dx - 1].astype(jnp.float32)
        total = total.astype(jnp.bfloat16)
        if dy == 0:
            out_ref[:, y] = total.reshape(SUBL, sub, rows)
            return None
        summed[dy - 1] = total
        return send(summed.at[dy - 1], homed.at[dy - 1], on_context(-dy * RING))

    swap0 = multiply(0)
    low[1].wait_recv()
    swap1 = multiply(1)
    cross0 = pair(0, swap0)
    high[1].wait_recv()
    swap3 = multiply(3)
    cross1 = pair(1, swap1)
    finish(0, cross0)
    for copy in across:
        copy.wait_recv()
    swap2 = multiply(2)
    cross3 = pair(3, swap3)
    home1 = finish(1, cross1)
    cross2 = pair(2, swap2)
    home3 = finish(3, cross3)
    home2 = finish(2, cross2)
    for dy, copy in ((1, home1), (3, home3), (2, home2)):
        copy.wait_recv()
        out_ref[:, lax.rem(y + dy, SPLIT)] = homed[dy - 1].reshape(SUBL, sub, rows)
    for copy in started:
        copy.wait_send()


def per_device(q_proj, k_proj, v_proj, short_filter, residue, decay_rate, out_weight):
    rows, chans = q_proj.shape
    modes = residue.shape[0]
    taps = short_filter.shape[1]
    group_width = chans // short_filter.shape[2]
    sub = out_weight.shape[0] // SPLIT
    share = SUBL * sub
    filters = jnp.repeat(
        short_filter.astype(jnp.float32).reshape(3 * taps, -1), group_width, axis=1
    )
    f32, bf16 = jnp.float32, jnp.bfloat16
    scratch = [
        ((rows + SUBL, LANES), f32),
        ((2 * SUBL, chans), f32),
        ((rows * SUBL, LANES), f32),
        ((rows * SUBL, LANES), f32),
        ((rows * SUBL, LANES), f32),
        ((3, modes * SUBL, LANES), f32),
        ((SUBL, chans), f32),
        ((SUBL, chans), f32),
        ((3, modes * SUBL, LANES), bf16),
        ((10, modes * SUBL, LANES), bf16),
        ((RING, SPLIT, sub, chans), bf16),
        ((SPLIT, 2, rows // 2, chans), bf16),
        ((SPLIT, 2, SPLIT, share, rows), bf16),
        ((SPLIT, SPLIT, share, rows), bf16),
        ((SPLIT, SPLIT, share, rows), bf16),
        ((SPLIT, SPLIT - 1, share, rows), bf16),
        ((SPLIT - 1, share, rows), bf16),
        ((SPLIT - 1, share, rows), bf16),
    ]
    result = pl.pallas_call(
        functools.partial(mixer_kernel, rows * lax.axis_size("context")),
        out_shape=jax.ShapeDtypeStruct((SUBL, SPLIT, sub, rows), bf16),
        in_specs=[pl.BlockSpec(memory_space=pltpu.VMEM)] * 7,
        out_specs=pl.BlockSpec(memory_space=pltpu.VMEM),
        scratch_shapes=[pltpu.VMEM(shape, kind) for shape, kind in scratch]
        + [pltpu.SemaphoreType.DMA((COPIES,))] * 2,
        compiler_params=pltpu.CompilerParams(
            collective_id=0, has_side_effects=True, vmem_limit_bytes=48 * 1024 * 1024
        ),
    )(
        q_proj, k_proj, v_proj, filters, residue, decay_rate,
        out_weight.reshape(SPLIT, sub, chans),
    )
    return result.reshape(SUBL * SPLIT * sub, rows)


def solution(mesh):
    return jax.shard_map(
        per_device,
        mesh=mesh,
        in_specs=(
            P("context", "tensor"),
            P("context", "tensor"),
            P("context", "tensor"),
            P(None, None, "tensor"),
            P(None, "tensor"),
            P(None, "tensor"),
            P("context", "tensor"),
        ),
        out_specs=P("tensor", "context"),
        check_vma=False,
    )
```

time: 514 us -> 95.9 us (0.19)
  waiting for transfers between devices: 325 us -> 0 us
  Pallas kernels: 0 us -> 88.1 us
  matrix products: 53.2 us -> 0 us
  other arithmetic: 51.9 us -> 0 us
  local copies, waits for them, and re-layouts: 54.5 us -> 6.28 us
  between operations: 13.4 us -> 0.04 us
  starting transfers between devices: 11.6 us -> 0 us
    all_gather x3 -> x0, waiting for transfers between devices: 285 us -> none  [the longest x2 236 us: prefix(): gathered = jax.tree.map(lambda a: lax.all_gather(a, axis), part)]
    pallas_call x0 -> x1, Pallas kernels: none -> 88.1 us  [per_device(): pl.pallas_call(functools.partial(mixer_kernel, rows * lax.axis_size('cont...]
    dot_general x5 -> x0, matrix products: 53.2 us -> none  [the longest x1 18 us: per_device(): jnp.einsum('qmc,smc->qsc', prior * mode_scale[None], lead_powers, precisi...]
    add x59 -> x0, other arithmetic: 46.2 us -> none  [the longest x54 43.8 us: compose(): return (earlier[0] * later[0], earlier[1] * later[0] + later[1])]
    reduce_scatter x1 -> x0, waiting for transfers between devices: 38.5 us -> none  [per_device(): lax.psum_scatter(partial_terms.astype(jnp.bfloat16), 'tensor', scatter_di...]
    exp x2 -> x0, local copies, waits for them, and re-layouts: 12.3 us -> none  [the longest x1 6.17 us: per_device(): jnp.exp(-decay_step[None] * (sub_len - 1 - offsets)[:, None, None])]
    dot_general x2 -> x0, local copies, waits for them, and re-layouts: 11.5 us -> none  [the longest x1 6.32 us: per_device(): jnp.einsum('sto,oc->stc', jnp.asarray(one_hot), intra_kernel, precision=l...]
    ppermute x3 -> x0, starting transfers between devices: 11.4 us -> none  [passed_along(): return lax.ppermute(block, axis, route)]
  transfers between devices with their start and end apart: 7 -> 0, of which waited for: 4 -> 0; matrix products, arithmetic and copies ran while one was open for 29% -> 0% of each run, Pallas kernels for 0% -> 0%
where the time goes in v2:
time: 95.9 us; the launch traced here: 94.4 us
  Pallas kernels  88.1 us (92%)
  local copies, waits for them, and re-layouts  6.28 us (7%)
    pallas_call x1, Pallas kernels, per_device(): pl.pallas_call(functools.partial(mixer_kernel, rows * lax.axis_size('cont...  88.1 us
    unnamed x13, local copies, waits for them, and re-layouts  5.24 us

profile of v2, /device:TPU:24, one launch (start us, length us, event | category | flops | bytes accessed | tf_op | source)
XLA Modules:
  0.0 94.4 jit_solution(12381856151113184595)
XLA Ops:
  0.0 0.0 copy-start
  0.0 0.8 reshape.21
  0.8 0.1 broadcast_in_dim.3
  0.9 0.0 copy-start.3
  0.9 0.2 reshape.17.filt_ref
  1.1 0.0 copy-done
  1.1 0.8 copy-done.3
  1.8 0.0 copy-start.1
  1.8 1.0 %copy-done.1 = bf16[256,1024]{1,0:T(8,128)(2,1)S(1)} copy-done((bf16[256,1024]{1,0:T(8,128)(2,1)S(1)}, bf16[256,1024]{1,0:T(8,128)(2,1)}, u32[]{:S(2)}) %copy-start.1) | copy-done | bytes 524312
  2.9 0.0 copy-start.2
  2.9 1.0 %copy-done.2 = bf16[256,1024]{1,0:T(8,128)(2,1)S(1)} copy-done((bf16[256,1024]{1,0:T(8,128)(2,1)S(1)}, bf16[256,1024]{1,0:T(8,128)(2,1)}, u32[]{:S(2)}) %copy-start.2) | copy-done | bytes 524312
  3.9 0.0 copy-start.4
  3.9 0.8 copy-done.4
  4.8 0.0 copy-start.5
  4.8 0.8 copy-done.5
  5.6 88.1 %shard_map.73 = bf16[8,4,16,256]{3,2,1,0:T(8,128)(2,1)S(1)} custom-call(bf16[256,1024]{1,0:T(8,128)(2,1)S(1)} %copy-done, bf16[256,1024]{1,0:T(8,128)(2,1)S(1)} %copy-done.1, bf16[256,1024]{1,0:T(8,128)(2,1)S(1)} %copy-done.2, f32[9,1024]{1,0:T(8,128)S(1)} %reshape.17.filt_ref, f32[16,1024]{1,0:T(8,128)S(1)} %copy-done.4, f32[16,1024]{1,0:T(8,128)S(1)} %copy-done.5, ...), custom_call_target="tpu_custom_call" | custom-call | tf_op jit(solution)/shard_map/pallas_call | solution.py:311
  93.7 0.7 copy.9
Async XLA Ops:
  0.0 1.1 %copy-start = (bf16[256,1024]{1,0:T(8,128)(2,1)S(1)}, bf16[256,1024]{1,0:T(8,128)(2,1)}, u32[]{:S(2)}) copy-start(bf16[256,1024]{1,0:T(8,128)(2,1)} %q_ref.1) | copy-start | bytes 1572868
  0.9 0.9 %copy-start.3 = (bf16[64,1024]{1,0:T(8,128)(2,1)S(1)}, bf16[64,1024]{1,0:T(8,128)(2,1)}, u32[]{:S(2)}) copy-start(bf16[64,1024]{1,0:T(8,128)(2,1)} %param.13) | copy-start | bytes 393220
  1.8 1.0 %copy-start.1 = (bf16[256,1024]{1,0:T(8,128)(2,1)S(1)}, bf16[256,1024]{1,0:T(8,128)(2,1)}, u32[]{:S(2)}) copy-start(bf16[256,1024]{1,0:T(8,128)(2,1)} %k_ref.1) | copy-start | bytes 1572868
  2.9 1.0 %copy-start.2 = (bf16[256,1024]{1,0:T(8,128)(2,1)S(1)}, bf16[256,1024]{1,0:T(8,128)(2,1)}, u32[]{:S(2)}) copy-start(bf16[256,1024]{1,0:T(8,128)(2,1)} %v_ref.1) | copy-start | bytes 1572868
  3.9 0.8 copy-start.4
  4.8 0.8 copy-start.5

commit v3 on v2

--- a/solution.py
+++ b/solution.py
@@ -11,15 +11,14 @@
 RING = 16
 LANES = 128
 SUBL = 8
-UP, DOWN = 6, 9
-FAR = (1, 2, 3, 4, 8, 12)
+UP, DOWN = 7, 8
 COPIES = 128
 
 
 def mixer_kernel(
-    total_rows, q_ref, k_ref, v_ref, filt_ref, residue_ref, rate_ref, w_ref, out_ref,
-    ext, head, p3, q3, g3, wide, rim_out, rim_in, st_out, st_in, whole, tokens,
-    part, swapped, paired, crossed, summed, homed, send_sem, recv_sem,
+    total_rows, q_hbm, k_hbm, v_hbm, short_hbm, residue_hbm, rate_hbm, w_hbm, out_ref,
+    q_ref, k_ref, v_ref, short_ref, residue_ref, rate_ref, w_ref, filt_ref, ext, head, p3, q3, g3, wide, rim_out, rim_in, st_out, st_in, whole, tokens,
+    part, swapped, paired, crossed, summed, homed, send_sem, recv_sem, load_sem,
 ):
     rows = q_ref.shape[0]
     modes = rate_ref.shape[0]
@@ -40,13 +39,21 @@
         return {"tensor": lax.rem(seat + 2 * distance, 2 * SPLIT)}
 
     other_core = {"tensor": x * 2 + (1 - core)}
-    peers = [on_context(d) for d in FAR] + [on_context(-d) for d in FAR]
+    peers = [on_context(1), on_context(-1)]
     peers += [on_context(d * RING) for d in range(1, SPLIT)]
     peers += [on_ring(1), on_ring(-1), other_core]
     peers += [on_x(d) for d in range(1, SPLIT)]
     barrier = pltpu.get_barrier_semaphore()
     for peer in peers:
         pl.semaphore_signal(barrier, inc=1, device_id=peer, device_id_type=pl.DeviceIdType.MESH)
+
+    loads = []
+    for src, dst in (
+        (k_hbm, k_ref), (v_hbm, v_ref), (q_hbm, q_ref), (short_hbm, short_ref),
+        (rate_hbm, rate_ref), (residue_hbm, residue_ref), (w_hbm, w_ref),
+    ):
+        loads.append(pltpu.make_async_copy(src, dst, load_sem.at[len(loads)]))
+        loads[-1].start()
 
     started = []
 
@@ -64,6 +71,17 @@
         started.append(copy)
         return copy
 
+    taps, groups = short_ref.shape[1:]
+    chans = q_ref.shape[1]
+    owner = lax.broadcasted_iota(jnp.int32, (groups, chans), 1) // (chans // groups)
+    own = owner == lax.broadcasted_iota(jnp.int32, (groups, chans), 0)
+    spreader = jnp.where(own, 1.0, 0.0).astype(jnp.bfloat16)
+    for load in loads:
+        load.wait()
+    for n in range(3):
+        filt_ref[n, 0:taps, :] = lax.dot_general(
+            short_ref[n], spreader, (((1,), (0,)), ((), ())), preferred_element_type=jnp.float32
+        )
     rim_out[...] = jnp.zeros_like(rim_out)
     for n, src in enumerate((q_ref, k_ref, v_ref)):
         rim_out[2 * n : 2 * n + 2, :] = src[rows - 16 : rows, :].astype(jnp.float32)[14:16]
@@ -71,9 +89,9 @@
     def feature(which, src, lanes):
         ext[0:SUBL, :] = jnp.zeros((SUBL, LANES), jnp.float32)
         ext[SUBL : SUBL + rows, :] = src[:, lanes].astype(jnp.float32)
-        total = filt_ref[3 * which : 3 * which + 1, lanes] * ext[SUBL : SUBL + rows, :]
+        total = filt_ref[which, 0:1, lanes] * ext[SUBL : SUBL + rows, :]
         for tap in range(1, 3):
-            total = total + filt_ref[3 * which + tap : 3 * which + tap + 1, lanes] * ext[
+            total = total + filt_ref[which, tap : tap + 1, lanes] * ext[
                 SUBL - tap : SUBL - tap + rows, :
             ]
         return total.astype(jnp.bfloat16).astype(jnp.float32)
@@ -153,9 +171,9 @@
         head[0:SUBL, :] = jnp.zeros((SUBL, head.shape[1]), jnp.float32)
         head[SUBL - 2 : SUBL, :] = rim[2 * n : 2 * n + 2]
         head[SUBL : 2 * SUBL, :] = src[0:16, :].astype(jnp.float32)[0:SUBL]
-        total = filt_ref[3 * n : 3 * n + 1, :] * head[SUBL : 2 * SUBL, :]
+        total = filt_ref[n, 0:1, :] * head[SUBL : 2 * SUBL, :]
         for tap in range(1, 3):
-            total = total + filt_ref[3 * n + tap : 3 * n + tap + 1, :] * head[
+            total = total + filt_ref[n, tap : tap + 1, :] * head[
                 SUBL - tap : 2 * SUBL - tap, :
             ]
         feats.append(total.astype(jnp.bfloat16).astype(jnp.float32))
@@ -167,39 +185,52 @@
     head_end = jnp.concatenate(run(0, SUBL, (zero,) * modes, False), axis=0)
     state = jnp.concatenate(body_end, axis=0) + jnp.exp(-decay_step * (rows - SUBL)) * head_end
 
-    def start_round(slot, first_copy, distances):
-        return [
-            send(st_out.at[slot], st_in.at[first_copy + i], on_context(d))
-            for i, d in enumerate(distances)
-        ]
-
-    def end_round(copies, first_copy, distances, lead, total):
-        for i, d in enumerate(distances):
-            copies[i].wait_recv()
-            came = jnp.where(place >= d, st_in[first_copy + i].astype(jnp.float32), 0.0)
-            if d != lead:
-                came = came * jnp.exp(-decay_step * (rows * (d - lead)))
-            total = came if total is None else total + came
-        return total
-
+    half = RING // 2
     st_out[0] = state.astype(jnp.bfloat16)
-    near = (1, 2, 3, 4)
-    copies = start_round(0, 0, near)
-    ring(0)
-    ring(1)
-    state = end_round(copies, 0, near, 1, None)
-    st_out[1] = state.astype(jnp.bfloat16)
-    middle = (4, 8, 12)
-    copies = start_round(1, 4, middle)
-    ring(2)
-    ring(3)
-    ring(4)
-    state = end_round(copies, 4, middle, 0, state)
-    st_out[2] = state.astype(jnp.bfloat16)
-    distant = (16, 32, 48)
-    copies = start_round(2, 7, distant)
-    ring(5)
-    state = end_round(copies, 7, distant, 0, state)
+    carried = {
+        (1, 1): send(st_out.at[0], st_in.at[0], on_ring(1)),
+        (-1, 1): send(st_out.at[0], st_in.at[half], on_ring(-1)),
+    }
+    before = jnp.zeros_like(state)
+    after = state * jnp.exp(-decay_step * (rows * (RING - 1)))
+
+    def turn(lap, before, after):
+        for sign, count in ((1, half), (-1, half - 1)):
+            if lap > count:
+                continue
+            slot = lap - 1 if sign > 0 else half + lap - 1
+            carried[sign, lap].wait_recv()
+            if lap < count:
+                carried[sign, lap + 1] = send(st_in.at[slot], st_in.at[slot + 1], on_ring(sign))
+        for sign, count in ((1, half), (-1, half - 1)):
+            if lap > count:
+                continue
+            slot = lap - 1 if sign > 0 else half + lap - 1
+            distance = lap if sign > 0 else RING - lap
+            came = st_in[slot].astype(jnp.float32)
+            if distance > 1:
+                came = came * jnp.exp(-decay_step * (rows * (distance - 1)))
+            earlier = z >= distance
+            before = before + jnp.where(earlier, came, 0.0)
+            after = after + jnp.where(earlier, 0.0, came)
+        return before, after
+
+    for lap in range(1, half + 1):
+        before, after = turn(lap, before, after)
+        if lap % 4:
+            ring(lap - 1 - lap // 4)
+    st_out[1] = (after + jnp.exp(-decay_step * (rows * RING)) * before).astype(jnp.bfloat16)
+    rows_after = [
+        send(st_out.at[1], st_in.at[RING - 2 + d], on_context(d * RING)) for d in range(1, SPLIT)
+    ]
+    ring(6)
+    state = before
+    for d in range(1, SPLIT):
+        rows_after[d - 1].wait_recv()
+        came = jnp.where(y >= d, st_in[RING - 2 + d].astype(jnp.float32), 0.0)
+        if d > 1:
+            came = came * jnp.exp(-decay_step * (rows * RING * (d - 1)))
+        state = state + came
 
     run(0, rows, tuple(state[m * SUBL : (m + 1) * SUBL] for m in range(modes)), True)
     for g in range(SUBL):
@@ -210,14 +241,13 @@
     from_below, from_above = on_context(RING), on_context(-RING)
     low = [send(tokens.at[0, h], tokens.at[1, h], from_below) for h in (0, 1)]
     high = [send(tokens.at[0, h], tokens.at[3, h], from_above) for h in (1, 0)]
-    ring(6)
     ring(7)
     low[0].wait_recv()
     across = [send(tokens.at[1, 0], tokens.at[2, 0], from_below)]
     high[0].wait_recv()
     across.append(send(tokens.at[3, 1], tokens.at[2, 1], from_above))
     ring(8)
-    ring(9)
+
 
     share = SUBL * sub
 
@@ -280,15 +310,18 @@
 def per_device(q_proj, k_proj, v_proj, short_filter, residue, decay_rate, out_weight):
     rows, chans = q_proj.shape
     modes = residue.shape[0]
-    taps = short_filter.shape[1]
-    group_width = chans // short_filter.shape[2]
     sub = out_weight.shape[0] // SPLIT
     share = SUBL * sub
-    filters = jnp.repeat(
-        short_filter.astype(jnp.float32).reshape(3 * taps, -1), group_width, axis=1
-    )
     f32, bf16 = jnp.float32, jnp.bfloat16
     scratch = [
+        ((rows, chans), bf16),
+        ((rows, chans), bf16),
+        ((rows, chans), bf16),
+        (short_filter.shape, bf16),
+        (residue.shape, f32),
+        (decay_rate.shape, f32),
+        ((SPLIT, sub, chans), bf16),
+        ((3, SUBL, chans), f32),
         ((rows + SUBL, LANES), f32),
         ((2 * SUBL, chans), f32),
         ((rows * SUBL, LANES), f32),
@@ -297,8 +330,8 @@
         ((3, modes * SUBL, LANES), f32),
         ((SUBL, chans), f32),
         ((SUBL, chans), f32),
-        ((3, modes * SUBL, LANES), bf16),
-        ((10, modes * SUBL, LANES), bf16),
+        ((2, modes * SUBL, LANES), bf16),
+        ((RING + 2, modes * SUBL, LANES), bf16),
         ((RING, SPLIT, sub, chans), bf16),
         ((SPLIT, 2, rows // 2, chans), bf16),
         ((SPLIT, 2, SPLIT, share, rows), bf16),
@@ -311,15 +344,16 @@
     result = pl.pallas_call(
         functools.partial(mixer_kernel, rows * lax.axis_size("context")),
         out_shape=jax.ShapeDtypeStruct((SUBL, SPLIT, sub, rows), bf16),
-        in_specs=[pl.BlockSpec(memory_space=pltpu.VMEM)] * 7,
+        in_specs=[pl.BlockSpec(memory_space=pl.ANY)] * 7,
         out_specs=pl.BlockSpec(memory_space=pltpu.VMEM),
         scratch_shapes=[pltpu.VMEM(shape, kind) for shape, kind in scratch]
-        + [pltpu.SemaphoreType.DMA((COPIES,))] * 2,
+        + [pltpu.SemaphoreType.DMA((COPIES,))] * 2
+        + [pltpu.SemaphoreType.DMA((7,))],
         compiler_params=pltpu.CompilerParams(
-            collective_id=0, has_side_effects=True, vmem_limit_bytes=48 * 1024 * 1024
+            collective_id=0, has_side_effects=True, vmem_limit_bytes=60 * 1024 * 1024
         ),
     )(
-        q_proj, k_proj, v_proj, filters, residue, decay_rate,
+        q_proj, k_proj, v_proj, short_filter, residue, decay_rate,
         out_weight.reshape(SPLIT, sub, chans),
     )
     return result.reshape(SUBL * SPLIT * sub, rows)

time: 95.9 us -> 87 us (0.907)
  local copies, waits for them, and re-layouts: 6.28 us -> 1.67 us
  Pallas kernels: 88.1 us -> 84.7 us
    unnamed x13 -> x1, local copies, waits for them, and re-layouts: 5.24 us -> 1.67 us
    pallas_call x1, Pallas kernels: 88.1 us -> 84.7 us  [per_device(): pl.pallas_call(functools.partial(mixer_kernel, rows * lax.axis_size('cont...]
where the time goes in v3:
time: 87 us; the launch traced here: 86.4 us
  Pallas kernels  84.7 us (97%)
  local copies, waits for them, and re-layouts  1.67 us (2%)
    pallas_call x1, Pallas kernels, per_device(): pl.pallas_call(functools.partial(mixer_kernel, rows * lax.axis_size('cont...  84.7 us

profile of v3, /device:TPU:24, one launch (start us, length us, event | category | flops | bytes accessed | tf_op | source)
XLA Modules:
  0.0 86.4 jit_solution(11548055567959805528)
XLA Ops:
  0.0 84.7 %shard_map.73 = bf16[8,4,16,256]{3,2,1,0:T(8,128)(2,1)} custom-call(bf16[256,1024]{1,0:T(8,128)(2,1)} %q_hbm.1, bf16[256,1024]{1,0:T(8,128)(2,1)} %k_hbm.1, bf16[256,1024]{1,0:T(8,128)(2,1)} %v_hbm.1, bf16[3,3,64]{2,1,0:T(4,128)(2,1)} %short_hbm.1, f32[16,1024]{1,0:T(8,128)} %residue_hbm.1, f32[16,1024]{1,0:T(8,128)} %rate_hbm.1, bf16[4,16,1024]{2,1,0:T(8,128)(2,1)} %bitcast.3), custom_call_target="tpu_custom_call" | custom-call | tf_op jit(solution)/shard_map/pallas_call | solution.py:344
  84.8 1.7 %copy.9 = bf16[512,256]{1,0:T(8,128)(2,1)} copy(bf16[512,256]{1,0:T(8,128)(2,1)} %bitcast.2) | data formatting | bytes 524288

commit v4 on v3

--- a/solution.py
+++ b/solution.py
@@ -285,17 +285,17 @@
         return send(summed.at[dy - 1], homed.at[dy - 1], on_context(-dy * RING))
 
     swap0 = multiply(0)
+    cross0 = pair(0, swap0)
     low[1].wait_recv()
     swap1 = multiply(1)
-    cross0 = pair(0, swap0)
+    cross1 = pair(1, swap1)
     high[1].wait_recv()
     swap3 = multiply(3)
-    cross1 = pair(1, swap1)
     finish(0, cross0)
+    cross3 = pair(3, swap3)
     for copy in across:
         copy.wait_recv()
     swap2 = multiply(2)
-    cross3 = pair(3, swap3)
     home1 = finish(1, cross1)
     cross2 = pair(2, swap2)
     home3 = finish(3, cross3)

time: 87 us -> 87 us (level)
  no operation moved by 1% of the time
where the time goes in v4:
time: 87 us; the launch traced here: 85.8 us
  Pallas kernels  84.1 us (97%)
  local copies, waits for them, and re-layouts  1.67 us (2%)
    pallas_call x1, Pallas kernels, per_device(): pl.pallas_call(functools.partial(mixer_kernel, rows * lax.axis_size('cont...  84.1 us

profile of v4, /device:TPU:24, one launch (start us, length us, event | category | flops | bytes accessed | tf_op | source)
XLA Modules:
  0.0 85.8 jit_solution(7332520568865544611)
XLA Ops:
  0.0 84.1 %shard_map.73 = bf16[8,4,16,256]{3,2,1,0:T(8,128)(2,1)} custom-call(bf16[256,1024]{1,0:T(8,128)(2,1)} %q_hbm.1, bf16[256,1024]{1,0:T(8,128)(2,1)} %k_hbm.1, bf16[256,1024]{1,0:T(8,128)(2,1)} %v_hbm.1, bf16[3,3,64]{2,1,0:T(4,128)(2,1)} %short_hbm.1, f32[16,1024]{1,0:T(8,128)} %residue_hbm.1, f32[16,1024]{1,0:T(8,128)} %rate_hbm.1, bf16[4,16,1024]{2,1,0:T(8,128)(2,1)} %bitcast.3), custom_call_target="tpu_custom_call" | custom-call | tf_op jit(solution)/shard_map/pallas_call | solution.py:344
  84.1 1.7 %copy.9 = bf16[512,256]{1,0:T(8,128)(2,1)} copy(bf16[512,256]{1,0:T(8,128)(2,1)} %bitcast.2) | data formatting | bytes 524288
